TPU v7x, 32 devices: a whole 2x2x4 slice. The times are simulated.
32 devices in a mesh: seq: 4 (over x, core), head: 4 (over z), rep: 2 (over y).
Axes of the slice: x: 2, y: 2, z: 4, core: 2. Of those that a mesh axis runs over, the one named last changes fastest.
Arguments:
- queries: bfloat16 [8, 512, 3072], P(('seq', 'rep'), 'head'), may hold values from -18 to 18, as said below
- keys: bfloat16 [8, 512, 3072], P(('seq', 'rep'), 'head'), may hold values from -18 to 18, as said below
- values: bfloat16 [8, 512, 3072], P(('seq', 'rep'), 'head'), may hold values from -6 to 6
- text_kv: bfloat16 [8, 384, 6144], P(('seq', 'rep'), 'head'), may hold values from -18 to 18, as said below
- cotangent: bfloat16 [8, 512, 3072], P(('seq', 'rep'), None, 'head'), may hold values from -6 to 6
Outputs:
- attended: bfloat16 [8, 512, 3072], P(('seq', 'rep'), None, 'head')
- text_grad: bfloat16 [8, 384, 6144], P(('seq', 'rep'), 'head')
Inputs may be any that keep to these rules, and one draw needn't show every extreme that they name: `queries`: normal-like entries of order one. `keys`: normal-like entries of order one. `text_kv`: normal-like entries of order one.
All inputs are finite; a program needn't handle non-finite values.
Results may differ from a plain program's by a relative error of at most 0.007.
Values may be sent and summed in bfloat16 or wider, within the bound.
No kernel may reach another device: no remote copies, remote signals or barrier semaphores. Data moves between devices by JAX's collectives and lax.ppermute only.
A program may use at most 64 MiB of HBM per device.

v0:
```python
import jax
import jax.numpy as jnp
from jax import lax
from jax.experimental import pallas as pl
from jax.experimental.pallas import tpu as pltpu
from jax.sharding import PartitionSpec as P


HD = 128


def dot_nt(a, b):
    return lax.dot_general(a, b, (((1,), (1,)), ((), ())), preferred_element_type=jnp.float32)


def dot_nn(a, b):
    return lax.dot_general(a, b, (((1,), (0,)), ((), ())), preferred_element_type=jnp.float32)


def softmax_columns(scores):
    top = jnp.max(scores, axis=0, keepdims=True)
    weights = jnp.exp(scores - top)
    return weights / jnp.sum(weights, axis=0, keepdims=True)


def gather_queries(order, query_refs, query_all):
    rows = query_refs[0].shape[0]
    for at, ref in enumerate(query_refs):
        query_all[pl.ds(pl.multiple_of(order[at] * rows, rows), rows), :] = ref[...]


def cross_kernel(count, order, *refs):
    query_refs = refs[:count]
    text_refs = refs[count : 2 * count]
    grad_ref = refs[2 * count]
    out_ref = refs[2 * count + 1]
    piece_refs = refs[2 * count + 2 : 3 * count + 2]
    query_all = refs[3 * count + 2]
    scale = float(HD) ** (-0.5)
    gather_queries(order, query_refs, query_all)
    query = query_all[...]
    grad = grad_ref[...]
    text = jnp.concatenate([ref[...] for ref in text_refs], axis=0)
    text_keys = text[:, :HD]
    text_values = text[:, HD:]
    probs = softmax_columns(dot_nt(text_keys, query) * scale)
    rounded = probs.astype(jnp.bfloat16)
    dprobs = dot_nt(text_values, grad)
    dscores = probs * (dprobs - jnp.sum(dprobs * probs, axis=0, keepdims=True))
    dscores = dscores.astype(jnp.bfloat16)
    grad_keys = (dot_nn(dscores, query) * scale).astype(jnp.bfloat16)
    grad_values = dot_nn(rounded, grad).astype(jnp.bfloat16)
    rows = text_refs[0].shape[0]
    for at, ref in enumerate(piece_refs):
        ref[:, :HD] = grad_keys[at * rows : (at + 1) * rows]
        ref[:, HD:] = grad_values[at * rows : (at + 1) * rows]
    out_ref[...] = dot_nn(text_values.T, rounded).T


def self_kernel(count, order, *refs):
    query_refs = refs[:count]
    key_refs = refs[count : 2 * count]
    value_refs = refs[2 * count : 3 * count]
    cross_ref = refs[3 * count]
    out_ref = refs[3 * count + 1]
    query_all = refs[3 * count + 2]
    scale = float(HD) ** (-0.5)
    gather_queries(order, query_refs, query_all)
    keys = jnp.concatenate([ref[...] for ref in key_refs], axis=0)
    values = jnp.concatenate([ref[...] for ref in value_refs], axis=0).T
    length = query_all.shape[0]
    block = 512 if length % 512 == 0 else length
    for start in range(0, length, block):
        rows = pl.ds(start, block)
        probs = softmax_columns(dot_nt(keys, query_all[rows, :]) * scale).astype(jnp.bfloat16)
        out_ref[rows, :] = (dot_nn(values, probs).T + cross_ref[rows, :]).astype(jnp.bfloat16)


def column_block(rows, width):
    return pl.BlockSpec((rows, width), lambda head, order: (0, head))


def cross_call(order, query_pieces, text_pieces, cotangent):
    count = len(query_pieces)
    length, width = cotangent.shape
    heads = width // HD
    rows = query_pieces[0].shape[0]
    text_rows = text_pieces[0].shape[0]
    piece = jax.ShapeDtypeStruct(text_pieces[0].shape, jnp.bfloat16)
    return pl.pallas_call(
        lambda *refs: cross_kernel(count, *refs),
        name="cross",
        out_shape=[jax.ShapeDtypeStruct((length, width), jnp.float32)] + [piece] * count,
        grid_spec=pltpu.PrefetchScalarGridSpec(
            num_scalar_prefetch=1,
            grid=(heads,),
            in_specs=[column_block(rows, HD)] * count
            + [column_block(text_rows, 2 * HD)] * count
            + [column_block(length, HD)],
            out_specs=[column_block(length, HD)] + [column_block(text_rows, 2 * HD)] * count,
            scratch_shapes=[pltpu.VMEM((length, HD), jnp.bfloat16)],
        ),
    )(order, *query_pieces, *text_pieces, cotangent)


def self_call(order, query_pieces, key_pieces, value_pieces, cross_out):
    count = len(query_pieces)
    length, width = cross_out.shape
    heads = width // HD
    rows = query_pieces[0].shape[0]
    return pl.pallas_call(
        lambda *refs: self_kernel(count, *refs),
        name="self",
        out_shape=jax.ShapeDtypeStruct((length, width), jnp.bfloat16),
        grid_spec=pltpu.PrefetchScalarGridSpec(
            num_scalar_prefetch=1,
            grid=(heads,),
            in_specs=[column_block(rows, HD)] * (3 * count) + [column_block(length, HD)],
            out_specs=column_block(length, HD),
            scratch_shapes=[pltpu.VMEM((length, HD), jnp.bfloat16)],
        ),
    )(order, *query_pieces, *key_pieces, *value_pieces, cross_out)


def place_kernel(count, order, *refs):
    pieces = refs[:count]
    out_ref = refs[count]
    sems = refs[count + 1]
    width = pieces[0].shape[1]
    copies = [
        pltpu.make_async_copy(
            piece,
            out_ref.at[:, pl.ds(pl.multiple_of(order[at] * width, width), width)],
            sems.at[at],
        )
        for at, piece in enumerate(pieces)
    ]
    for copy in copies:
        copy.start()
    for copy in copies:
        copy.wait()


def place_call(order, pieces):
    count = len(pieces)
    rows, width = pieces[0].shape
    return pl.pallas_call(
        lambda *refs: place_kernel(count, *refs),
        name="place",
        out_shape=jax.ShapeDtypeStruct((rows, width * count), pieces[0].dtype),
        in_specs=[pl.BlockSpec(memory_space=pltpu.SMEM)]
        + [pl.BlockSpec(memory_space=pltpu.VMEM)] * count,
        out_specs=pl.BlockSpec(memory_space=pl.ANY),
        scratch_shapes=[pltpu.SemaphoreType.DMA((count,))],
    )(order, *[pltpu.with_memory_space_constraint(piece, pltpu.VMEM) for piece in pieces])


def send_order(count):
    near, far = [1], list(range(count - 1, 1, -1))
    first = [(name, step) for step in far[:1] for name in ("query", "text")]
    first += [(name, step) for step in near for name in ("query", "text", "key", "value")]
    later = [(name, step) for name in ("query", "text") for step in far[1:]]
    later += [(name, step) for name in ("key", "value") for step in far]
    return first + later


def solution(mesh):
    count = mesh.shape["head"]
    paired = count & (count - 1) == 0

    def target(index, step):
        return index ^ step if paired else (index + step) % count

    def origin(index, step):
        return index ^ step if paired else (index - step) % count

    def per_device(queries, keys, values, text_kv, cotangent):
        here = lax.axis_index("head")
        order = jnp.stack([origin(here, step) for step in range(count)]).astype(jnp.int32)
        goal = jnp.stack([target(here, step) for step in range(count)]).astype(jnp.int32)
        arrays = {"query": queries[0], "text": text_kv[0], "key": keys[0], "value": values[0]}

        def columns(name, step):
            rows, width = arrays[name].shape
            width //= count
            at = target(here, step) * width
            return lax.dynamic_slice(arrays[name], (0, at), (rows, width))

        got = {name: [columns(name, 0)] + [None] * (count - 1) for name in arrays}
        for name, step in sends:
            got[name][step] = lax.ppermute(
                columns(name, step),
                "head",
                [(index, target(index, step)) for index in range(count)],
            )
        cross_out, *grad_pieces = cross_call(order, got["query"], got["text"], cotangent[0])
        back = [grad_pieces[0]]
        for step in range(1, count):
            back.append(
                lax.ppermute(
                    grad_pieces[step],
                    "head",
                    [(target(index, step), index) for index in range(count)],
                )
            )
        attended = self_call(order, got["query"], got["key"], got["value"], cross_out)
        text_grad = place_call(goal, back)
        return attended[None], text_grad[None]

    sends = send_order(count)

    placed = (
        P(("seq", "rep"), "head", None),
        P(("seq", "rep"), "head", None),
        P(("seq", "rep"), "head", None),
        P(("seq", "rep"), "head", None),
        P(("seq", "rep"), None, "head"),
    )
    return jax.shard_map(
        per_device,
        mesh=mesh,
        in_specs=placed,
        out_specs=(P(("seq", "rep"), None, "head"), P(("seq", "rep"), "head", None)),
        check_vma=False,
    )
```

profile of v0, /device:TPU:0, one launch (start us, length us, event | category | flops | bytes accessed | tf_op | source)
XLA Modules:
  0.0 122.3 jit_solution(13905085477510504550)
XLA Ops:
  0.6 0.0 copy-start.1
  0.7 2.0 %dynamic-slice_bitcast_fusion.12 = (bf16[128,768]{1,0:T(8,128)(2,1)S(1)}, bf16[128,768]{1,0:T(8,128)(2,1)S(1)}, bf16[128,768]{1,0:T(8,128)(2,1)}, bf16[128,768]{1,0:T(8,128)(2,1)S(1)}) fusion(bf16[1,128,3072]{2,1,0:T(8,128)(2,1)} %param.5, s32[]{:T(128)S(6)} %select_n.35, s32[]{:T(128)S(6)} %select_n.33, s32[]{:T(128)S(6)} %select_n.32, s32[]{:T(128)S(6)} %select_n.34), kind=kLoop, calls=%fused_computation.12 | loop fusion | bytes 1572880 | tf_op jit(solution)/shard_map/dynamic_slice | solution.py:187
  2.7 3.1 %collective-permute-start = (bf16[128,768]{1,0:T(8,128)(2,1)S(1)}, bf16[128,768]{1,0:T(8,128)(2,1)S(1)}, u32[]{:S(2)}, u32[]{:S(2)}) collective-permute-start(bf16[128,768]{1,0:T(8,128)(2,1)S(1)} %get-tuple-element.25), channel_id=1, source_target_pairs={{0,2},{2,0},{4,6},{6,4},{1,3},{3,1},{5,7},{7,5},{8,10},{10,8},{12,... | collective-permute-start | bytes 589832 | tf_op jit(solution)/shard_map/ppermute | solution.py:191
  5.8 2.6 %collective-permute-start.1 = (bf16[128,768]{1,0:T(8,128)(2,1)S(1)}, bf16[128,768]{1,0:T(8,128)(2,1)S(1)}, u32[]{:S(2)}, u32[]{:S(2)}) collective-permute-start(bf16[128,768]{1,0:T(8,128)(2,1)S(1)} %get-tuple-element.27), channel_id=1, source_target_pairs={{0,4},{2,6},{4,0},{6,2},{1,5},{3,7},{5,1},{7,3},{8,12},{10,14},{12... | collective-permute-start | bytes 589832 | tf_op jit(solution)/shard_map/ppermute | solution.py:191
  8.3 0.0 collective-permute-start.2
  8.3 0.0 copy-done.1
  8.4 0.8 dynamic-slice_bitcast_fusion
  9.2 1.9 %collective-permute-start.10 = (bf16[96,1536]{1,0:T(8,128)(2,1)S(1)}, bf16[96,1536]{1,0:T(8,128)(2,1)S(1)}, u32[]{:S(2)}, u32[]{:S(2)}) collective-permute-start(bf16[96,1536]{1,0:T(8,128)(2,1)S(1)} %get-tuple-element.15), channel_id=1, source_target_pairs={{0,4},{2,6},{4,0},{6,2},{1,5},{3,7},{5,1},{7,3},{8,12},{10,14},{12... | collective-permute-start | bytes 884744 | tf_op jit(solution)/shard_map/ppermute | solution.py:191
  11.1 1.9 %collective-permute-start.11 = (bf16[96,1536]{1,0:T(8,128)(2,1)S(1)}, bf16[96,1536]{1,0:T(8,128)(2,1)S(1)}, u32[]{:S(2)}, u32[]{:S(2)}) collective-permute-start(bf16[96,1536]{1,0:T(8,128)(2,1)S(1)} %get-tuple-element.12), channel_id=1, source_target_pairs={{0,6},{2,4},{4,2},{6,0},{1,7},{3,5},{5,3},{7,1},{8,14},{10,12},{12... | collective-permute-start | bytes 884744 | tf_op jit(solution)/shard_map/ppermute | solution.py:191
  13.0 1.2 collective-permute-done.refs_2_
  14.1 0.0 collective-permute-start.9
  14.1 0.0 copy-done.5
  14.1 0.9 dynamic-slice_bitcast_fusion.8
  15.0 20.6 %collective-permute-done.1.refs_3_ = bf16[128,768]{1,0:T(8,128)(2,1)S(1)} collective-permute-done((bf16[128,768]{1,0:T(8,128)(2,1)S(1)}, bf16[128,768]{1,0:T(8,128)(2,1)S(1)}, u32[]{:S(2)}, u32[]{:S(2)}) %collective-permute-start.1) | collective-permute-done | bytes 196640 | tf_op jit(solution)/shard_map/ppermute | solution.py:191
  35.6 0.0 collective-permute-start.3
  35.6 0.0 collective-permute-done.2.refs_4_
  35.6 0.0 copy-start.4
  35.6 5.8 %collective-permute-start.4 = (bf16[128,768]{1,0:T(8,128)(2,1)S(1)}, bf16[128,768]{1,0:T(8,128)(2,1)S(1)}, u32[]{:S(2)}, u32[]{:S(2)}) collective-permute-start(bf16[128,768]{1,0:T(8,128)(2,1)S(1)} %get-tuple-element.23), channel_id=1, source_target_pairs={{0,4},{2,6},{4,0},{6,2},{1,5},{3,7},{5,1},{7,3},{8,12},{10,14},{12... | collective-permute-start | bytes 589832 | tf_op jit(solution)/shard_map/ppermute | solution.py:191
  41.4 0.0 copy-done.6
  41.4 0.8 dynamic-slice_bitcast_fusion.4
  42.1 0.0 copy-done.2
  42.1 10.3 %collective-permute-done.10.refs_7_ = bf16[96,1536]{1,0:T(8,128)(2,1)S(1)} collective-permute-done((bf16[96,1536]{1,0:T(8,128)(2,1)S(1)}, bf16[96,1536]{1,0:T(8,128)(2,1)S(1)}, u32[]{:S(2)}, u32[]{:S(2)}) %collective-permute-start.10) | collective-permute-done | bytes 294944 | tf_op jit(solution)/shard_map/ppermute | solution.py:191
  52.5 2.5 %collective-permute-start.5 = (bf16[128,768]{1,0:T(8,128)(2,1)S(1)}, bf16[128,768]{1,0:T(8,128)(2,1)S(1)}, u32[]{:S(2)}, u32[]{:S(2)}) collective-permute-start(bf16[128,768]{1,0:T(8,128)(2,1)S(1)} %get-tuple-element.20), channel_id=1, source_target_pairs={{0,6},{2,4},{4,2},{6,0},{1,7},{3,5},{5,3},{7,1},{8,14},{10,12},{12... | collective-permute-start | bytes 589832 | tf_op jit(solution)/shard_map/ppermute | solution.py:191
  55.0 0.0 collective-permute-done.11.refs_8_
  55.0 6.5 %collective-permute-start.6 = (bf16[128,768]{1,0:T(8,128)(2,1)S(1)}, bf16[128,768]{1,0:T(8,128)(2,1)S(1)}, u32[]{:S(2)}, u32[]{:S(2)}) collective-permute-start(bf16[128,768]{1,0:T(8,128)(2,1)S(1)} %get-tuple-element.17), channel_id=1, source_target_pairs={{0,2},{2,0},{4,6},{6,4},{1,3},{3,1},{5,7},{7,5},{8,10},{10,8},{12,... | collective-permute-start | bytes 589832 | tf_op jit(solution)/shard_map/ppermute | solution.py:191
  61.5 0.6 pad_add_fusion.refs_0_
  62.0 0.0 collective-permute-done.9.refs_6_
  62.0 0.0 copy-done.3
  62.1 0.7 copy-done.9
  62.7 9.6 %cross.1 = (f32[512,768]{1,0:T(8,128)}, bf16[96,1536]{1,0:T(8,128)(2,1)}, bf16[96,1536]{1,0:T(8,128)(2,1)}, bf16[96,1536]{1,0:T(8,128)(2,1)}, bf16[96,1536]{1,0:T(8,128)(2,1)}) custom-call(s32[4]{0:T(128)} %pad_add_fusion.refs_0_, bf16[128,768]{1,0:T(8,128)(2,1)} %get-tuple-element.26.refs_1_, bf16[128,768]{1,0:T(8,128)(2,1)} %copy-done.2, ...), custom_call_target="tpu_custom_call" | custom-call | tf_op jit(solution)/shard_map/cross/pallas_call | solution.py:90
  72.3 0.1 collective-permute-start.12
  72.4 0.0 collective-permute-done.3.refs_6_
  72.4 2.7 %collective-permute-start.13 = (bf16[96,1536]{1,0:T(8,128)(2,1)}, bf16[96,1536]{1,0:T(8,128)(2,1)S(1)}, u32[]{:S(2)}, u32[]{:S(2)}) collective-permute-start(bf16[96,1536]{1,0:T(8,128)(2,1)} %get-tuple-element.10), channel_id=1, source_target_pairs={{4,0},{6,2},{0,4},{2,6},{5,1},{7,3},{1,5},{3,7},{12,8},{14,10},{8,... | collective-permute-start | bytes 884744 | tf_op jit(solution)/shard_map/ppermute | solution.py:200
  75.1 0.0 collective-permute-done.4.refs_7_
  75.1 1.7 %collective-permute-start.14 = (bf16[96,1536]{1,0:T(8,128)(2,1)}, bf16[96,1536]{1,0:T(8,128)(2,1)S(1)}, u32[]{:S(2)}, u32[]{:S(2)}) collective-permute-start(bf16[96,1536]{1,0:T(8,128)(2,1)} %get-tuple-element.11), channel_id=1, source_target_pairs={{6,0},{4,2},{2,4},{0,6},{7,1},{5,3},{3,5},{1,7},{14,8},{12,10},{10... | collective-permute-start | bytes 884744 | tf_op jit(solution)/shard_map/ppermute | solution.py:200
  76.8 0.0 collective-permute-done.5.refs_8_
  76.8 0.0 collective-permute-start.7
  76.8 0.0 collective-permute-done.6.refs_10_
  76.8 2.2 %collective-permute-start.8 = (bf16[128,768]{1,0:T(8,128)(2,1)S(1)}, bf16[128,768]{1,0:T(8,128)(2,1)S(1)}, u32[]{:S(2)}, u32[]{:S(2)}) collective-permute-start(bf16[128,768]{1,0:T(8,128)(2,1)S(1)} %get-tuple-element.16), channel_id=1, source_target_pairs={{0,6},{2,4},{4,2},{6,0},{1,7},{3,5},{5,3},{7,1},{8,14},{10,12},{12... | collective-permute-start | bytes 589832 | tf_op jit(solution)/shard_map/ppermute | solution.py:191
  79.0 32.3 %collective-permute-done.7.refs_11_ = bf16[128,768]{1,0:T(8,128)(2,1)S(1)} collective-permute-done((bf16[128,768]{1,0:T(8,128)(2,1)S(1)}, bf16[128,768]{1,0:T(8,128)(2,1)S(1)}, u32[]{:S(2)}, u32[]{:S(2)}) %collective-permute-start.7) | collective-permute-done | bytes 196640 | tf_op jit(solution)/shard_map/ppermute | solution.py:191
  111.3 0.0 collective-permute-done.8.refs_12_
  111.3 0.6 copy-done.14
  112.0 0.1 copy-done.15
  112.0 8.5 %self.1 = bf16[512,768]{1,0:T(8,128)(2,1)} custom-call(s32[4]{0:T(128)} %pad_add_fusion.refs_0_, bf16[128,768]{1,0:T(8,128)(2,1)} %get-tuple-element.26.refs_1_, bf16[128,768]{1,0:T(8,128)(2,1)} %copy-done.2, bf16[128,768]{1,0:T(8,128)(2,1)} %copy-done.3, bf16[128,768]{1,0:T(8,128)(2,1)} %copy-done.4, bf16[128,768]{1,0:T(8,128)(2,1)} %get-tuple-element.22.refs_5_, ...), custom_call_target="tpu_custom_call" | custom-call | tf_op jit(solution)/shard_map/self/pallas_call | solution.py:111
  120.6 0.0 collective-permute-done.12.refs_2_
  120.6 0.0 collective-permute-done.13.refs_3_
  120.6 0.0 collective-permute-done.14.refs_4_
  120.6 1.7 %place.1 = bf16[96,6144]{1,0:T(8,128)(2,1)} custom-call(s32[4]{0:T(128)} %pad_add_fusion.refs_0_, bf16[96,1536]{1,0:T(8,128)(2,1)S(1)} %copy-done, bf16[96,1536]{1,0:T(8,128)(2,1)S(1)} %collective-permute-done.12.refs_2_, bf16[96,1536]{1,0:T(8,128)(2,1)S(1)} %collective-permute-done.13.refs_3_, bf16[96,1536]{1,0:T(8,128)(2,1)S(1)} %collective-permute-done.14.refs_4_), custom_call_target="tpu_custom_call" | custom-call | tf_op jit(solution)/shard_map/place/pallas_call | solution.py:147
  (22 shorter events, 0.0 us)
Async XLA Ops:
  0.6 7.7 %copy-start.1 = (bf16[1,96,6144]{2,1,0:T(8,128)(2,1)S(1)}, bf16[1,96,6144]{2,1,0:T(8,128)(2,1)}, u32[]{:S(2)}) copy-start(bf16[1,96,6144]{2,1,0:T(8,128)(2,1)} %param.8) | copy-start | bytes 3538948
  2.7 11.4 %collective-permute-start = (bf16[128,768]{1,0:T(8,128)(2,1)S(1)}, bf16[128,768]{1,0:T(8,128)(2,1)S(1)}, u32[]{:S(2)}, u32[]{:S(2)}) collective-permute-start(bf16[128,768]{1,0:T(8,128)(2,1)S(1)} %get-tuple-element.25), channel_id=1, source_target_pairs={{0,2},{2,0},{4,6},{6,4},{1,3},{3,1},{5,7},{7,5},{8,10},{10,8},{12,... | collective-permute-start | bytes 589832 | tf_op jit(solution)/shard_map/ppermute | solution.py:191
  5.8 29.8 %collective-permute-start.1 = (bf16[128,768]{1,0:T(8,128)(2,1)S(1)}, bf16[128,768]{1,0:T(8,128)(2,1)S(1)}, u32[]{:S(2)}, u32[]{:S(2)}) collective-permute-start(bf16[128,768]{1,0:T(8,128)(2,1)S(1)} %get-tuple-element.27), channel_id=1, source_target_pairs={{0,4},{2,6},{4,0},{6,2},{1,5},{3,7},{5,1},{7,3},{8,12},{10,14},{12... | collective-permute-start | bytes 589832 | tf_op jit(solution)/shard_map/ppermute | solution.py:191
  8.3 27.2 %collective-permute-start.2 = (bf16[128,768]{1,0:T(8,128)(2,1)S(1)}, bf16[128,768]{1,0:T(8,128)(2,1)S(1)}, u32[]{:S(2)}, u32[]{:S(2)}) collective-permute-start(bf16[128,768]{1,0:T(8,128)(2,1)S(1)} %get-tuple-element.24), channel_id=1, source_target_pairs={{0,6},{2,4},{4,2},{6,0},{1,7},{3,5},{5,3},{7,1},{8,14},{10,12},{12... | collective-permute-start | bytes 589832 | tf_op jit(solution)/shard_map/ppermute | solution.py:191
  8.4 5.8 %copy-start.5 = (bf16[1,128,3072]{2,1,0:T(8,128)(2,1)S(1)}, bf16[1,128,3072]{2,1,0:T(8,128)(2,1)}, u32[]{:S(2)}) copy-start(bf16[1,128,3072]{2,1,0:T(8,128)(2,1)} %param.6) | copy-start | bytes 2359300
  9.1 32.2 %copy-start.6 = (bf16[1,128,3072]{2,1,0:T(8,128)(2,1)S(1)}, bf16[1,128,3072]{2,1,0:T(8,128)(2,1)}, u32[]{:S(2)}) copy-start(bf16[1,128,3072]{2,1,0:T(8,128)(2,1)} %param.7) | copy-start | bytes 2359300
  9.2 43.3 %collective-permute-start.10 = (bf16[96,1536]{1,0:T(8,128)(2,1)S(1)}, bf16[96,1536]{1,0:T(8,128)(2,1)S(1)}, u32[]{:S(2)}, u32[]{:S(2)}) collective-permute-start(bf16[96,1536]{1,0:T(8,128)(2,1)S(1)} %get-tuple-element.15), channel_id=1, source_target_pairs={{0,4},{2,6},{4,0},{6,2},{1,5},{3,7},{5,1},{7,3},{8,12},{10,14},{12... | collective-permute-start | bytes 884744 | tf_op jit(solution)/shard_map/ppermute | solution.py:191
  11.1 43.9 %collective-permute-start.11 = (bf16[96,1536]{1,0:T(8,128)(2,1)S(1)}, bf16[96,1536]{1,0:T(8,128)(2,1)S(1)}, u32[]{:S(2)}, u32[]{:S(2)}) collective-permute-start(bf16[96,1536]{1,0:T(8,128)(2,1)S(1)} %get-tuple-element.12), channel_id=1, source_target_pairs={{0,6},{2,4},{4,2},{6,0},{1,7},{3,5},{5,3},{7,1},{8,14},{10,12},{12... | collective-permute-start | bytes 884744 | tf_op jit(solution)/shard_map/ppermute | solution.py:191
  14.1 28.0 %copy-start.2 = (bf16[128,768]{1,0:T(8,128)(2,1)}, bf16[128,768]{1,0:T(8,128)(2,1)S(1)}, u32[]{:S(2)}) copy-start(bf16[128,768]{1,0:T(8,128)(2,1)S(1)} %collective-permute-done.refs_2_) | copy-start | bytes 589828
  14.1 47.9 %collective-permute-start.9 = (bf16[96,1536]{1,0:T(8,128)(2,1)S(1)}, bf16[96,1536]{1,0:T(8,128)(2,1)S(1)}, u32[]{:S(2)}, u32[]{:S(2)}) collective-permute-start(bf16[96,1536]{1,0:T(8,128)(2,1)S(1)} %get-tuple-element.13), channel_id=1, source_target_pairs={{0,2},{2,0},{4,6},{6,4},{1,3},{3,1},{5,7},{7,5},{8,10},{10,8},{12,... | collective-permute-start | bytes 884744 | tf_op jit(solution)/shard_map/ppermute | solution.py:191
  35.6 26.5 %copy-start.3 = (bf16[128,768]{1,0:T(8,128)(2,1)}, bf16[128,768]{1,0:T(8,128)(2,1)S(1)}, u32[]{:S(2)}) copy-start(bf16[128,768]{1,0:T(8,128)(2,1)S(1)} %collective-permute-done.1.refs_3_) | copy-start | bytes 589828
  35.6 36.8 %collective-permute-start.3 = (bf16[128,768]{1,0:T(8,128)(2,1)}, bf16[128,768]{1,0:T(8,128)(2,1)S(1)}, u32[]{:S(2)}, u32[]{:S(2)}) collective-permute-start(bf16[128,768]{1,0:T(8,128)(2,1)} %get-tuple-element.21), channel_id=1, source_target_pairs={{0,2},{2,0},{4,6},{6,4},{1,3},{3,1},{5,7},{7,5},{8,10},{10,8},{12,... | collective-permute-start | bytes 589832 | tf_op jit(solution)/shard_map/ppermute | solution.py:191
  35.6 26.4 %copy-start.4 = (bf16[128,768]{1,0:T(8,128)(2,1)}, bf16[128,768]{1,0:T(8,128)(2,1)S(1)}, u32[]{:S(2)}) copy-start(bf16[128,768]{1,0:T(8,128)(2,1)S(1)} %collective-permute-done.2.refs_4_) | copy-start | bytes 589828
  35.6 39.5 %collective-permute-start.4 = (bf16[128,768]{1,0:T(8,128)(2,1)S(1)}, bf16[128,768]{1,0:T(8,128)(2,1)S(1)}, u32[]{:S(2)}, u32[]{:S(2)}) collective-permute-start(bf16[128,768]{1,0:T(8,128)(2,1)S(1)} %get-tuple-element.23), channel_id=1, source_target_pairs={{0,4},{2,6},{4,0},{6,2},{1,5},{3,7},{5,1},{7,3},{8,12},{10,14},{12... | collective-permute-start | bytes 589832 | tf_op jit(solution)/shard_map/ppermute | solution.py:191
  52.5 9.6 %copy-start.7 = (bf16[96,1536]{1,0:T(8,128)(2,1)}, bf16[96,1536]{1,0:T(8,128)(2,1)S(1)}, u32[]{:S(2)}) copy-start(bf16[96,1536]{1,0:T(8,128)(2,1)S(1)} %collective-permute-done.10.refs_7_) | copy-start | bytes 884740
  52.5 24.3 %collective-permute-start.5 = (bf16[128,768]{1,0:T(8,128)(2,1)S(1)}, bf16[128,768]{1,0:T(8,128)(2,1)S(1)}, u32[]{:S(2)}, u32[]{:S(2)}) collective-permute-start(bf16[128,768]{1,0:T(8,128)(2,1)S(1)} %get-tuple-element.20), channel_id=1, source_target_pairs={{0,6},{2,4},{4,2},{6,0},{1,7},{3,5},{5,3},{7,1},{8,14},{10,12},{12... | collective-permute-start | bytes 589832 | tf_op jit(solution)/shard_map/ppermute | solution.py:191
  55.0 7.1 %copy-start.8 = (bf16[96,1536]{1,0:T(8,128)(2,1)}, bf16[96,1536]{1,0:T(8,128)(2,1)S(1)}, u32[]{:S(2)}) copy-start(bf16[96,1536]{1,0:T(8,128)(2,1)S(1)} %collective-permute-done.11.refs_8_) | copy-start | bytes 884740
  55.0 21.9 %collective-permute-start.6 = (bf16[128,768]{1,0:T(8,128)(2,1)S(1)}, bf16[128,768]{1,0:T(8,128)(2,1)S(1)}, u32[]{:S(2)}, u32[]{:S(2)}) collective-permute-start(bf16[128,768]{1,0:T(8,128)(2,1)S(1)} %get-tuple-element.17), channel_id=1, source_target_pairs={{0,2},{2,0},{4,6},{6,4},{1,3},{3,1},{5,7},{7,5},{8,10},{10,8},{12,... | collective-permute-start | bytes 589832 | tf_op jit(solution)/shard_map/ppermute | solution.py:191
  62.0 0.7 copy-start.9
  72.3 48.2 %collective-permute-start.12 = (bf16[96,1536]{1,0:T(8,128)(2,1)}, bf16[96,1536]{1,0:T(8,128)(2,1)S(1)}, u32[]{:S(2)}, u32[]{:S(2)}) collective-permute-start(bf16[96,1536]{1,0:T(8,128)(2,1)} %get-tuple-element.9), channel_id=1, source_target_pairs={{2,0},{0,2},{6,4},{4,6},{3,1},{1,3},{7,5},{5,7},{10,8},{8,10},{14,... | collective-permute-start | bytes 884744 | tf_op jit(solution)/shard_map/ppermute | solution.py:200
  72.4 38.9 %copy-start.10 = (bf16[128,768]{1,0:T(8,128)(2,1)}, bf16[128,768]{1,0:T(8,128)(2,1)S(1)}, u32[]{:S(2)}) copy-start(bf16[128,768]{1,0:T(8,128)(2,1)S(1)} %collective-permute-done.3.refs_6_) | copy-start | bytes 589828
  72.4 48.1 %collective-permute-start.13 = (bf16[96,1536]{1,0:T(8,128)(2,1)}, bf16[96,1536]{1,0:T(8,128)(2,1)S(1)}, u32[]{:S(2)}, u32[]{:S(2)}) collective-permute-start(bf16[96,1536]{1,0:T(8,128)(2,1)} %get-tuple-element.10), channel_id=1, source_target_pairs={{4,0},{6,2},{0,4},{2,6},{5,1},{7,3},{1,5},{3,7},{12,8},{14,10},{8,... | collective-permute-start | bytes 884744 | tf_op jit(solution)/shard_map/ppermute | solution.py:200
  75.1 36.2 %copy-start.11 = (bf16[128,768]{1,0:T(8,128)(2,1)}, bf16[128,768]{1,0:T(8,128)(2,1)S(1)}, u32[]{:S(2)}) copy-start(bf16[128,768]{1,0:T(8,128)(2,1)S(1)} %collective-permute-done.4.refs_7_) | copy-start | bytes 589828
  75.1 45.5 %collective-permute-start.14 = (bf16[96,1536]{1,0:T(8,128)(2,1)}, bf16[96,1536]{1,0:T(8,128)(2,1)S(1)}, u32[]{:S(2)}, u32[]{:S(2)}) collective-permute-start(bf16[96,1536]{1,0:T(8,128)(2,1)} %get-tuple-element.11), channel_id=1, source_target_pairs={{6,0},{4,2},{2,4},{0,6},{7,1},{5,3},{3,5},{1,7},{14,8},{12,10},{10... | collective-permute-start | bytes 884744 | tf_op jit(solution)/shard_map/ppermute | solution.py:200
  76.8 34.5 %copy-start.12 = (bf16[128,768]{1,0:T(8,128)(2,1)}, bf16[128,768]{1,0:T(8,128)(2,1)S(1)}, u32[]{:S(2)}) copy-start(bf16[128,768]{1,0:T(8,128)(2,1)S(1)} %collective-permute-done.5.refs_8_) | copy-start | bytes 589828
  76.8 34.5 %collective-permute-start.7 = (bf16[128,768]{1,0:T(8,128)(2,1)S(1)}, bf16[128,768]{1,0:T(8,128)(2,1)S(1)}, u32[]{:S(2)}, u32[]{:S(2)}) collective-permute-start(bf16[128,768]{1,0:T(8,128)(2,1)S(1)} %get-tuple-element.19), channel_id=1, source_target_pairs={{0,4},{2,6},{4,0},{6,2},{1,5},{3,7},{5,1},{7,3},{8,12},{10,14},{12... | collective-permute-start | bytes 589832 | tf_op jit(solution)/shard_map/ppermute | solution.py:191
  76.8 34.5 %copy-start.13 = (bf16[128,768]{1,0:T(8,128)(2,1)}, bf16[128,768]{1,0:T(8,128)(2,1)S(1)}, u32[]{:S(2)}) copy-start(bf16[128,768]{1,0:T(8,128)(2,1)S(1)} %collective-permute-done.6.refs_10_) | copy-start | bytes 589828
  76.8 34.5 %collective-permute-start.8 = (bf16[128,768]{1,0:T(8,128)(2,1)S(1)}, bf16[128,768]{1,0:T(8,128)(2,1)S(1)}, u32[]{:S(2)}, u32[]{:S(2)}) collective-permute-start(bf16[128,768]{1,0:T(8,128)(2,1)S(1)} %get-tuple-element.16), channel_id=1, source_target_pairs={{0,6},{2,4},{4,2},{6,0},{1,7},{3,5},{5,3},{7,1},{8,14},{10,12},{12... | collective-permute-start | bytes 589832 | tf_op jit(solution)/shard_map/ppermute | solution.py:191
  111.3 0.7 copy-start.14
  111.3 0.7 copy-start.15
  112.0 8.5 %copy-start = (bf16[96,1536]{1,0:T(8,128)(2,1)S(1)}, bf16[96,1536]{1,0:T(8,128)(2,1)}, u32[]{:S(2)}) copy-start(bf16[96,1536]{1,0:T(8,128)(2,1)} %get-tuple-element.8.refs_1_) | copy-start | bytes 884740
where the time goes:
time: 123 us; the launch traced here: 122 us
  waiting for transfers between devices  64.3 us (52%)
  starting transfers between devices  30.9 us (25%)
  Pallas kernels  19.8 us (16%)
  local copies, waits for them, and re-layouts  5.91 us (5%)
    ppermute x12, waiting for transfers between devices, per_device(): lax.ppermute(columns(name, step), 'head', [(index, target(index, step)) f...  64.3 us
    ppermute x12, starting transfers between devices, per_device(): lax.ppermute(columns(name, step), 'head', [(index, target(index, step)) f...  26.4 us
    pallas_call x1, Pallas kernels, cross_call(): pl.pallas_call(lambda *refs: cross_kernel(count, *refs), name='cross', ou...  9.59 us
    pallas_call x1, Pallas kernels, self_call(): pl.pallas_call(lambda *refs: self_kernel(count, *refs), name='self', out_...  8.5 us
    dynamic_slice x4, local copies, waits for them, and re-layouts, columns(): return lax.dynamic_slice(arrays[name], (0, at), (rows, width))  4.46 us
    ppermute x3, starting transfers between devices, per_device(): lax.ppermute(grad_pieces[step], 'head', [(target(index, step), index) for...  4.45 us
  transfers between devices with their start and end apart: 15, of which 4 were waited for; matrix products, arithmetic and copies ran while one was open for 2% of the time, Pallas kernels for 15%

commit v1 on v0

--- a/solution.py
+++ b/solution.py
@@ -57,23 +57,27 @@
     out_ref[...] = dot_nn(text_values.T, rounded).T
 
 
-def self_kernel(count, order, *refs):
+def scores_kernel(count, order, *refs):
     query_refs = refs[:count]
     key_refs = refs[count : 2 * count]
-    value_refs = refs[2 * count : 3 * count]
-    cross_ref = refs[3 * count]
-    out_ref = refs[3 * count + 1]
-    query_all = refs[3 * count + 2]
+    probs_ref = refs[2 * count]
     scale = float(HD) ** (-0.5)
-    gather_queries(order, query_refs, query_all)
     keys = jnp.concatenate([ref[...] for ref in key_refs], axis=0)
-    values = jnp.concatenate([ref[...] for ref in value_refs], axis=0).T
-    length = query_all.shape[0]
-    block = 512 if length % 512 == 0 else length
-    for start in range(0, length, block):
-        rows = pl.ds(start, block)
-        probs = softmax_columns(dot_nt(keys, query_all[rows, :]) * scale).astype(jnp.bfloat16)
-        out_ref[rows, :] = (dot_nn(values, probs).T + cross_ref[rows, :]).astype(jnp.bfloat16)
+    rows = query_refs[0].shape[0]
+    for at, ref in enumerate(query_refs):
+        scores = dot_nt(ref[...], keys) * scale
+        weights = jnp.exp(scores - jnp.max(scores, axis=1, keepdims=True))
+        probs = weights / jnp.sum(weights, axis=1, keepdims=True)
+        start = pl.multiple_of(order[at] * rows, rows)
+        probs_ref[pl.ds(start, rows), :] = probs.astype(jnp.bfloat16)
+
+
+def values_kernel(count, *refs):
+    value_refs = refs[:count]
+    probs_ref, cross_ref, out_ref = refs[count:]
+    values = jnp.concatenate([ref[...] for ref in value_refs], axis=0)
+    out = dot_nn(probs_ref[...], values)
+    out_ref[...] = (out + cross_ref[...]).astype(jnp.bfloat16)
 
 
 def column_block(rows, width):
@@ -103,37 +107,54 @@
     )(order, *query_pieces, *text_pieces, cotangent)
 
 
-def self_call(order, query_pieces, key_pieces, value_pieces, cross_out):
+def scores_call(order, query_pieces, key_pieces):
     count = len(query_pieces)
-    length, width = cross_out.shape
+    rows, width = query_pieces[0].shape
+    length = rows * count
     heads = width // HD
-    rows = query_pieces[0].shape[0]
-    return pl.pallas_call(
-        lambda *refs: self_kernel(count, *refs),
-        name="self",
-        out_shape=jax.ShapeDtypeStruct((length, width), jnp.bfloat16),
+    return pl.pallas_call(
+        lambda *refs: scores_kernel(count, *refs),
+        name="scores",
+        out_shape=jax.ShapeDtypeStruct((length, heads * length), jnp.bfloat16),
         grid_spec=pltpu.PrefetchScalarGridSpec(
             num_scalar_prefetch=1,
             grid=(heads,),
-            in_specs=[column_block(rows, HD)] * (3 * count) + [column_block(length, HD)],
-            out_specs=column_block(length, HD),
-            scratch_shapes=[pltpu.VMEM((length, HD), jnp.bfloat16)],
+            in_specs=[column_block(rows, HD)] * (2 * count),
+            out_specs=column_block(length, length),
         ),
-    )(order, *query_pieces, *key_pieces, *value_pieces, cross_out)
-
-
-def place_kernel(count, order, *refs):
-    pieces = refs[:count]
-    out_ref = refs[count]
-    sems = refs[count + 1]
+    )(order, *query_pieces, *key_pieces)
+
+
+def values_call(value_pieces, probs, cross_out):
+    count = len(value_pieces)
+    length, width = cross_out.shape
+    rows = value_pieces[0].shape[0]
+    heads = width // HD
+
+    def block(rows, width):
+        return pl.BlockSpec((rows, width), lambda head: (0, head))
+
+    return pl.pallas_call(
+        lambda *refs: values_kernel(count, *refs),
+        name="values",
+        out_shape=jax.ShapeDtypeStruct((length, width), jnp.bfloat16),
+        grid=(heads,),
+        in_specs=[block(rows, HD)] * count + [block(length, length), block(length, HD)],
+        out_specs=block(length, HD),
+    )(*value_pieces, probs, cross_out)
+
+
+def place_kernel(steps, order, *refs):
+    pieces = refs[: len(steps)]
+    out_ref, sems = refs[-2:]
     width = pieces[0].shape[1]
     copies = [
         pltpu.make_async_copy(
             piece,
-            out_ref.at[:, pl.ds(pl.multiple_of(order[at] * width, width), width)],
+            out_ref.at[:, pl.ds(pl.multiple_of(order[step] * width, width), width)],
             sems.at[at],
         )
-        for at, piece in enumerate(pieces)
+        for at, (step, piece) in enumerate(zip(steps, pieces))
     ]
     for copy in copies:
         copy.start()
@@ -141,18 +162,42 @@
         copy.wait()
 
 
-def place_call(order, pieces):
-    count = len(pieces)
+def place_call(order, steps, pieces, whole=None):
+    count = order.shape[0]
     rows, width = pieces[0].shape
-    return pl.pallas_call(
-        lambda *refs: place_kernel(count, *refs),
+    held = [] if whole is None else [whole]
+    return pl.pallas_call(
+        lambda *refs: place_kernel(steps, *refs),
         name="place",
         out_shape=jax.ShapeDtypeStruct((rows, width * count), pieces[0].dtype),
         in_specs=[pl.BlockSpec(memory_space=pltpu.SMEM)]
-        + [pl.BlockSpec(memory_space=pltpu.VMEM)] * count,
+        + [pl.BlockSpec(memory_space=pltpu.VMEM)] * len(steps)
+        + [pl.BlockSpec(memory_space=pl.ANY)] * len(held),
         out_specs=pl.BlockSpec(memory_space=pl.ANY),
-        scratch_shapes=[pltpu.SemaphoreType.DMA((count,))],
-    )(order, *[pltpu.with_memory_space_constraint(piece, pltpu.VMEM) for piece in pieces])
+        scratch_shapes=[pltpu.SemaphoreType.DMA((len(steps),))],
+        input_output_aliases={len(steps) + 1: 0} if held else {},
+    )(
+        order,
+        *[pltpu.with_memory_space_constraint(piece, pltpu.VMEM) for piece in pieces],
+        *held,
+    )
+
+
+def pick_call(array, at, width):
+    def pick_kernel(at, array_ref, out_ref, sem):
+        start = pl.multiple_of(at[0] * width, width)
+        copy = pltpu.make_async_copy(array_ref.at[:, pl.ds(start, width)], out_ref, sem)
+        copy.start()
+        copy.wait()
+
+    return pl.pallas_call(
+        pick_kernel,
+        name="pick",
+        out_shape=pltpu.VMEM((array.shape[0], width), array.dtype),
+        in_specs=[pl.BlockSpec(memory_space=pltpu.SMEM), pl.BlockSpec(memory_space=pl.ANY)],
+        out_specs=pl.BlockSpec(memory_space=pltpu.VMEM),
+        scratch_shapes=[pltpu.SemaphoreType.DMA],
+    )(at.reshape(1).astype(jnp.int32), array)
 
 
 def send_order(count):
@@ -186,10 +231,13 @@
             at = target(here, step) * width
             return lax.dynamic_slice(arrays[name], (0, at), (rows, width))
 
+        first, step = sends[0]
+        held = pick_call(arrays[first], target(here, step), arrays[first].shape[1] // count)
+        arrays[first], held = lax.optimization_barrier((arrays[first], held))
         got = {name: [columns(name, 0)] + [None] * (count - 1) for name in arrays}
-        for name, step in sends:
+        for at, (name, step) in enumerate(sends):
             got[name][step] = lax.ppermute(
-                columns(name, step),
+                columns(name, step) if at else held,
                 "head",
                 [(index, target(index, step)) for index in range(count)],
             )
@@ -203,8 +251,12 @@
                     [(target(index, step), index) for index in range(count)],
                 )
             )
-        attended = self_call(order, got["query"], got["key"], got["value"], cross_out)
-        text_grad = place_call(goal, back)
+        probs = scores_call(order, got["query"], got["key"])
+        attended = values_call(got["value"], probs, cross_out)
+        text_grad = place_call(goal, tuple(range(count - 1)), back[:-1])
+        last = back[-1]
+        at = target(here, count - 1) * last.shape[1]
+        text_grad = lax.dynamic_update_slice(text_grad, last, (0, at))
         return attended[None], text_grad[None]
 
     sends = send_order(count)

time: 123 us -> 122 us (level)
  waiting for transfers between devices: 64.3 us -> 57.7 us
  Pallas kernels: 19.8 us -> 25.2 us
    ppermute x12, waiting for transfers between devices: 64.3 us -> 57.7 us  [per_device(): lax.ppermute(columns(name, step) if at else held, 'head', [(index, target...]
    pallas_call x2 -> x4, Pallas kernels: 10.2 us -> 15.6 us  [the longest x1 6.88 us: scores_call(): pl.pallas_call(lambda *refs: scores_kernel(count, *refs), name='scores',...]
  transfers between devices with their start and end apart: 15 -> 15, of which waited for: 4 -> 4; matrix products, arithmetic and copies ran while one was open for 2% -> 3% of each run, Pallas kernels for 15% -> 20%
where the time goes in v1:
time: 122 us; the launch traced here: 121 us
  waiting for transfers between devices  57.7 us (47%)
  starting transfers between devices  30.4 us (25%)
  Pallas kernels  25.2 us (21%)
  local copies, waits for them, and re-layouts  5.95 us (5%)
    ppermute x12, waiting for transfers between devices, per_device(): lax.ppermute(columns(name, step) if at else held, 'head', [(index, target...  57.7 us
    ppermute x12, starting transfers between devices, per_device(): lax.ppermute(columns(name, step) if at else held, 'head', [(index, target...  26 us
    pallas_call x1, Pallas kernels, cross_call(): pl.pallas_call(lambda *refs: cross_kernel(count, *refs), name='cross', ou...  9.63 us
    pallas_call x1, Pallas kernels, scores_call(): pl.pallas_call(lambda *refs: scores_kernel(count, *refs), name='scores',...  6.88 us
    pallas_call x1, Pallas kernels, values_call(): pl.pallas_call(lambda *refs: values_kernel(count, *refs), name='values',...  6.01 us
    ppermute x3, starting transfers between devices, per_device(): lax.ppermute(grad_pieces[step], 'head', [(target(index, step), index) for...  4.44 us
    dynamic_slice x4, local copies, waits for them, and re-layouts, columns(): return lax.dynamic_slice(arrays[name], (0, at), (rows, width))  3.65 us
  transfers between devices with their start and end apart: 15, of which 4 were waited for; matrix products, arithmetic and copies ran while one was open for 3% of the time, Pallas kernels for 20%

profile of v1, /device:TPU:0, one launch (start us, length us, event | category | flops | bytes accessed | tf_op | source)
XLA Modules:
  0.0 120.8 jit_solution(11250979356440029361)
XLA Ops:
  0.7 1.1 pick.1
  1.8 0.1 copy-done.1
  1.9 0.9 constant_dynamic-slice_fusion
  2.7 3.1 %collective-permute-start.3 = (bf16[128,768]{1,0:T(8,128)(2,1)}, bf16[128,768]{1,0:T(8,128)(2,1)S(1)}, u32[]{:S(2)}, u32[]{:S(2)}) collective-permute-start(bf16[128,768]{1,0:T(8,128)(2,1)} %get-tuple-element.25), channel_id=1, source_target_pairs={{0,2},{2,0},{4,6},{6,4},{1,3},{3,1},{5,7},{7,5},{8,10},{10,8},{12,... | collective-permute-start | bytes 589832 | tf_op jit(solution)/shard_map/ppermute | solution.py:239
  5.8 2.6 %collective-permute-start.4 = (bf16[128,768]{1,0:T(8,128)(2,1)}, bf16[128,768]{1,0:T(8,128)(2,1)S(1)}, u32[]{:S(2)}, u32[]{:S(2)}) collective-permute-start(bf16[128,768]{1,0:T(8,128)(2,1)} %get-tuple-element.24), channel_id=1, source_target_pairs={{0,4},{2,6},{4,0},{6,2},{1,5},{3,7},{5,1},{7,3},{8,12},{10,14},{12... | collective-permute-start | bytes 589832 | tf_op jit(solution)/shard_map/ppermute | solution.py:239
  8.4 0.0 collective-permute-start.5
  8.4 0.0 copy-done.2
  8.4 1.0 dynamic-slice_bitcast_fusion
  9.4 1.9 %collective-permute-start.10 = (bf16[96,1536]{1,0:T(8,128)(2,1)}, bf16[96,1536]{1,0:T(8,128)(2,1)S(1)}, u32[]{:S(2)}, u32[]{:S(2)}) collective-permute-start(bf16[96,1536]{1,0:T(8,128)(2,1)} %get-tuple-element.19), channel_id=1, source_target_pairs={{0,4},{2,6},{4,0},{6,2},{1,5},{3,7},{5,1},{7,3},{8,12},{10,14},{12... | collective-permute-start | bytes 884744 | tf_op jit(solution)/shard_map/ppermute | solution.py:239
  11.3 1.9 %collective-permute-start.11 = (bf16[96,1536]{1,0:T(8,128)(2,1)}, bf16[96,1536]{1,0:T(8,128)(2,1)S(1)}, u32[]{:S(2)}, u32[]{:S(2)}) collective-permute-start(bf16[96,1536]{1,0:T(8,128)(2,1)} %get-tuple-element.16), channel_id=1, source_target_pairs={{0,6},{2,4},{4,2},{6,0},{1,7},{3,5},{5,3},{7,1},{8,14},{10,12},{12... | collective-permute-start | bytes 884744 | tf_op jit(solution)/shard_map/ppermute | solution.py:239
  13.2 1.1 collective-permute-done.3.refs_2_
  14.4 0.0 collective-permute-start.9
  14.4 1.0 dynamic-slice_bitcast_fusion.4
  15.4 20.4 %collective-permute-done.4.refs_3_ = bf16[128,768]{1,0:T(8,128)(2,1)S(1)} collective-permute-done((bf16[128,768]{1,0:T(8,128)(2,1)}, bf16[128,768]{1,0:T(8,128)(2,1)S(1)}, u32[]{:S(2)}, u32[]{:S(2)}) %collective-permute-start.4) | collective-permute-done | bytes 196640 | tf_op jit(solution)/shard_map/ppermute | solution.py:239
  35.8 0.0 collective-permute-start.6
  35.8 0.0 collective-permute-done.5.refs_4_
  35.8 0.0 copy-start.5
  35.8 5.8 %collective-permute-start.7 = (bf16[128,768]{1,0:T(8,128)(2,1)}, bf16[128,768]{1,0:T(8,128)(2,1)S(1)}, u32[]{:S(2)}, u32[]{:S(2)}) collective-permute-start(bf16[128,768]{1,0:T(8,128)(2,1)} %get-tuple-element.23), channel_id=1, source_target_pairs={{0,4},{2,6},{4,0},{6,2},{1,5},{3,7},{5,1},{7,3},{8,12},{10,14},{12... | collective-permute-start | bytes 589832 | tf_op jit(solution)/shard_map/ppermute | solution.py:239
  41.6 0.8 dynamic-slice_bitcast_fusion.8
  42.4 10.3 %collective-permute-done.10.refs_7_ = bf16[96,1536]{1,0:T(8,128)(2,1)S(1)} collective-permute-done((bf16[96,1536]{1,0:T(8,128)(2,1)}, bf16[96,1536]{1,0:T(8,128)(2,1)S(1)}, u32[]{:S(2)}, u32[]{:S(2)}) %collective-permute-start.10) | collective-permute-done | bytes 294944 | tf_op jit(solution)/shard_map/ppermute | solution.py:239
  52.7 2.5 %collective-permute-start.8 = (bf16[128,768]{1,0:T(8,128)(2,1)}, bf16[128,768]{1,0:T(8,128)(2,1)S(1)}, u32[]{:S(2)}, u32[]{:S(2)}) collective-permute-start(bf16[128,768]{1,0:T(8,128)(2,1)} %get-tuple-element.20), channel_id=1, source_target_pairs={{0,6},{2,4},{4,2},{6,0},{1,7},{3,5},{5,3},{7,1},{8,14},{10,12},{12... | collective-permute-start | bytes 589832 | tf_op jit(solution)/shard_map/ppermute | solution.py:239
  55.2 0.0 collective-permute-done.11.refs_8_
  55.2 6.5 %collective-permute-start = (bf16[128,768]{1,0:T(8,128)(2,1)S(1)}, bf16[128,768]{1,0:T(8,128)(2,1)S(1)}, u32[]{:S(2)}, u32[]{:S(2)}) collective-permute-start(bf16[128,768]{1,0:T(8,128)(2,1)S(1)} %get-tuple-element.28), channel_id=1, source_target_pairs={{0,2},{2,0},{4,6},{6,4},{1,3},{3,1},{5,7},{7,5},{8,10},{10,8},{12,... | collective-permute-start | bytes 589832 | tf_op jit(solution)/shard_map/ppermute | solution.py:239
  61.7 0.6 pad_add_fusion.refs_0_
  62.3 0.0 collective-permute-done.9.refs_6_
  62.4 0.7 copy-done.10
  63.1 9.6 %cross.1 = (f32[512,768]{1,0:T(8,128)}, bf16[96,1536]{1,0:T(8,128)(2,1)}, bf16[96,1536]{1,0:T(8,128)(2,1)}, bf16[96,1536]{1,0:T(8,128)(2,1)}, bf16[96,1536]{1,0:T(8,128)(2,1)}) custom-call(s32[4]{0:T(128)} %pad_add_fusion.refs_0_, bf16[128,768]{1,0:T(8,128)(2,1)} %get-tuple-element.26.refs_1_, bf16[128,768]{1,0:T(8,128)(2,1)} %copy-done.3, ...), custom_call_target="tpu_custom_call" | custom-call | tf_op jit(solution)/shard_map/cross/pallas_call | solution.py:94
  72.7 0.1 collective-permute-start.12
  72.8 0.0 collective-permute-done.6.refs_6_
  72.8 0.0 copy-start.11
  72.8 2.2 %collective-permute-start.13 = (bf16[96,1536]{1,0:T(8,128)(2,1)}, bf16[96,1536]{1,0:T(8,128)(2,1)S(1)}, u32[]{:S(2)}, u32[]{:S(2)}) collective-permute-start(bf16[96,1536]{1,0:T(8,128)(2,1)} %get-tuple-element.14), channel_id=1, source_target_pairs={{4,0},{6,2},{0,4},{2,6},{5,1},{7,3},{1,5},{3,7},{12,8},{14,10},{8,... | collective-permute-start | bytes 884744 | tf_op jit(solution)/shard_map/ppermute | solution.py:248
  75.0 0.0 collective-permute-done.7.refs_7_
  75.0 2.1 %collective-permute-start.14 = (bf16[96,1536]{1,0:T(8,128)(2,1)}, bf16[96,1536]{1,0:T(8,128)(2,1)S(1)}, u32[]{:S(2)}, u32[]{:S(2)}) collective-permute-start(bf16[96,1536]{1,0:T(8,128)(2,1)} %get-tuple-element.15), channel_id=1, source_target_pairs={{6,0},{4,2},{2,4},{0,6},{7,1},{5,3},{3,5},{1,7},{14,8},{12,10},{10... | collective-permute-start | bytes 884744 | tf_op jit(solution)/shard_map/ppermute | solution.py:248
  77.2 0.0 collective-permute-done.8.refs_8_
  77.2 0.0 collective-permute-start.1
  77.2 0.0 collective-permute-done.refs_1_
  77.2 1.8 %collective-permute-start.2 = (bf16[128,768]{1,0:T(8,128)(2,1)S(1)}, bf16[128,768]{1,0:T(8,128)(2,1)S(1)}, u32[]{:S(2)}, u32[]{:S(2)}) collective-permute-start(bf16[128,768]{1,0:T(8,128)(2,1)S(1)} %get-tuple-element.27), channel_id=1, source_target_pairs={{0,6},{2,4},{4,2},{6,0},{1,7},{3,5},{5,3},{7,1},{8,14},{10,12},{12... | collective-permute-start | bytes 589832 | tf_op jit(solution)/shard_map/ppermute | solution.py:239
  79.0 6.9 %scores.1.refs_4_ = bf16[512,3072]{1,0:T(8,128)(2,1)} custom-call(s32[4]{0:T(128)} %pad_add_fusion.refs_0_, bf16[128,768]{1,0:T(8,128)(2,1)} %get-tuple-element.26.refs_1_, bf16[128,768]{1,0:T(8,128)(2,1)} %copy-done.3, bf16[128,768]{1,0:T(8,128)(2,1)} %copy-done.4, bf16[128,768]{1,0:T(8,128)(2,1)} %copy-done.5, bf16[128,768]{1,0:T(8,128)(2,1)} %get-tuple-element.22.refs_5_, ...), custom_call_target="tpu_custom_call" | custom-call | tf_op jit(solution)/shard_map/scores/pallas_call | solution.py:115
  85.9 25.8 %collective-permute-done.1.refs_2_ = bf16[128,768]{1,0:T(8,128)(2,1)S(1)} collective-permute-done((bf16[128,768]{1,0:T(8,128)(2,1)S(1)}, bf16[128,768]{1,0:T(8,128)(2,1)S(1)}, u32[]{:S(2)}, u32[]{:S(2)}) %collective-permute-start.1) | collective-permute-done | bytes 196640 | tf_op jit(solution)/shard_map/ppermute | solution.py:239
  111.7 0.0 collective-permute-done.2.refs_3_
  111.7 0.7 copy-done.15
  112.3 0.1 copy-done.16
  112.4 6.0 %values.1 = bf16[512,768]{1,0:T(8,128)(2,1)} custom-call(bf16[128,768]{1,0:T(8,128)(2,1)} %get-tuple-element.29.refs_0_, bf16[128,768]{1,0:T(8,128)(2,1)} %copy-done.13, bf16[128,768]{1,0:T(8,128)(2,1)} %copy-done.15, bf16[128,768]{1,0:T(8,128)(2,1)} %copy-done.16, bf16[512,3072]{1,0:T(8,128)(2,1)} %scores.1.refs_4_, f32[512,768]{1,0:T(8,128)} %get-tuple-element.11.refs_5_), custom_call_target="tpu_custom_call" | custom-call | tf_op jit(solution)/shard_map/values/pallas_call | solution.py:137
  118.4 0.0 collective-permute-done.12.refs_2_
  118.4 0.0 collective-permute-done.13.refs_3_
  118.4 1.6 %place.1 = bf16[96,6144]{1,0:T(8,128)(2,1)} custom-call(s32[4]{0:T(128)} %pad_add_fusion.refs_0_, bf16[96,1536]{1,0:T(8,128)(2,1)S(1)} %copy-done, bf16[96,1536]{1,0:T(8,128)(2,1)S(1)} %collective-permute-done.12.refs_2_, bf16[96,1536]{1,0:T(8,128)(2,1)S(1)} %collective-permute-done.13.refs_3_), custom_call_target="tpu_custom_call" | custom-call | tf_op jit(solution)/shard_map/place/pallas_call | solution.py:169
  120.0 0.0 collective-permute-done.14
  120.0 0.7 bitcast_dynamic-update-slice_fusion
  (27 shorter events, 0.1 us)
Async XLA Ops:
  0.6 1.2 %copy-start.1 = (bf16[1,128,3072]{2,1,0:T(8,128)(2,1)S(1)}, bf16[1,128,3072]{2,1,0:T(8,128)(2,1)}, u32[]{:S(2)}) copy-start(bf16[1,128,3072]{2,1,0:T(8,128)(2,1)} %param.5) | copy-start | bytes 2359300
  0.6 7.7 %copy-start.2 = (bf16[1,96,6144]{2,1,0:T(8,128)(2,1)S(1)}, bf16[1,96,6144]{2,1,0:T(8,128)(2,1)}, u32[]{:S(2)}) copy-start(bf16[1,96,6144]{2,1,0:T(8,128)(2,1)} %param.8) | copy-start | bytes 3538948
  2.7 11.6 %collective-permute-start.3 = (bf16[128,768]{1,0:T(8,128)(2,1)}, bf16[128,768]{1,0:T(8,128)(2,1)S(1)}, u32[]{:S(2)}, u32[]{:S(2)}) collective-permute-start(bf16[128,768]{1,0:T(8,128)(2,1)} %get-tuple-element.25), channel_id=1, source_target_pairs={{0,2},{2,0},{4,6},{6,4},{1,3},{3,1},{5,7},{7,5},{8,10},{10,8},{12,... | collective-permute-start | bytes 589832 | tf_op jit(solution)/shard_map/ppermute | solution.py:239
  5.8 30.0 %collective-permute-start.4 = (bf16[128,768]{1,0:T(8,128)(2,1)}, bf16[128,768]{1,0:T(8,128)(2,1)S(1)}, u32[]{:S(2)}, u32[]{:S(2)}) collective-permute-start(bf16[128,768]{1,0:T(8,128)(2,1)} %get-tuple-element.24), channel_id=1, source_target_pairs={{0,4},{2,6},{4,0},{6,2},{1,5},{3,7},{5,1},{7,3},{8,12},{10,14},{12... | collective-permute-start | bytes 589832 | tf_op jit(solution)/shard_map/ppermute | solution.py:239
  8.4 27.5 %collective-permute-start.5 = (bf16[128,768]{1,0:T(8,128)(2,1)S(1)}, bf16[128,768]{1,0:T(8,128)(2,1)S(1)}, u32[]{:S(2)}, u32[]{:S(2)}) collective-permute-start(bf16[128,768]{1,0:T(8,128)(2,1)S(1)} %pick.1), channel_id=1, source_target_pairs={{0,6},{2,4},{4,2},{6,0},{1,7},{3,5},{5,3},{7,1},{8,14},{10,12},{12... | collective-permute-start | bytes 589832 | tf_op jit(solution)/shard_map/ppermute | solution.py:239
  8.4 6.0 %copy-start.6 = (bf16[1,128,3072]{2,1,0:T(8,128)(2,1)S(1)}, bf16[1,128,3072]{2,1,0:T(8,128)(2,1)}, u32[]{:S(2)}) copy-start(bf16[1,128,3072]{2,1,0:T(8,128)(2,1)} %param.6) | copy-start | bytes 2359300
  9.4 32.2 %copy-start.7 = (bf16[1,128,3072]{2,1,0:T(8,128)(2,1)S(1)}, bf16[1,128,3072]{2,1,0:T(8,128)(2,1)}, u32[]{:S(2)}) copy-start(bf16[1,128,3072]{2,1,0:T(8,128)(2,1)} %param.7) | copy-start | bytes 2359300
  9.4 43.3 %collective-permute-start.10 = (bf16[96,1536]{1,0:T(8,128)(2,1)}, bf16[96,1536]{1,0:T(8,128)(2,1)S(1)}, u32[]{:S(2)}, u32[]{:S(2)}) collective-permute-start(bf16[96,1536]{1,0:T(8,128)(2,1)} %get-tuple-element.19), channel_id=1, source_target_pairs={{0,4},{2,6},{4,0},{6,2},{1,5},{3,7},{5,1},{7,3},{8,12},{10,14},{12... | collective-permute-start | bytes 884744 | tf_op jit(solution)/shard_map/ppermute | solution.py:239
  11.3 43.9 %collective-permute-start.11 = (bf16[96,1536]{1,0:T(8,128)(2,1)}, bf16[96,1536]{1,0:T(8,128)(2,1)S(1)}, u32[]{:S(2)}, u32[]{:S(2)}) collective-permute-start(bf16[96,1536]{1,0:T(8,128)(2,1)} %get-tuple-element.16), channel_id=1, source_target_pairs={{0,6},{2,4},{4,2},{6,0},{1,7},{3,5},{5,3},{7,1},{8,14},{10,12},{12... | collective-permute-start | bytes 884744 | tf_op jit(solution)/shard_map/ppermute | solution.py:239
  14.4 28.0 %copy-start.3 = (bf16[128,768]{1,0:T(8,128)(2,1)}, bf16[128,768]{1,0:T(8,128)(2,1)S(1)}, u32[]{:S(2)}) copy-start(bf16[128,768]{1,0:T(8,128)(2,1)S(1)} %collective-permute-done.3.refs_2_) | copy-start | bytes 589828
  14.4 48.0 %collective-permute-start.9 = (bf16[96,1536]{1,0:T(8,128)(2,1)}, bf16[96,1536]{1,0:T(8,128)(2,1)S(1)}, u32[]{:S(2)}, u32[]{:S(2)}) collective-permute-start(bf16[96,1536]{1,0:T(8,128)(2,1)} %get-tuple-element.17), channel_id=1, source_target_pairs={{0,2},{2,0},{4,6},{6,4},{1,3},{3,1},{5,7},{7,5},{8,10},{10,8},{12,... | collective-permute-start | bytes 884744 | tf_op jit(solution)/shard_map/ppermute | solution.py:239
  35.8 26.5 %copy-start.4 = (bf16[128,768]{1,0:T(8,128)(2,1)}, bf16[128,768]{1,0:T(8,128)(2,1)S(1)}, u32[]{:S(2)}) copy-start(bf16[128,768]{1,0:T(8,128)(2,1)S(1)} %collective-permute-done.4.refs_3_) | copy-start | bytes 589828
  35.8 37.0 %collective-permute-start.6 = (bf16[128,768]{1,0:T(8,128)(2,1)}, bf16[128,768]{1,0:T(8,128)(2,1)S(1)}, u32[]{:S(2)}, u32[]{:S(2)}) collective-permute-start(bf16[128,768]{1,0:T(8,128)(2,1)} %get-tuple-element.21), channel_id=1, source_target_pairs={{0,2},{2,0},{4,6},{6,4},{1,3},{3,1},{5,7},{7,5},{8,10},{10,8},{12,... | collective-permute-start | bytes 589832 | tf_op jit(solution)/shard_map/ppermute | solution.py:239
  35.8 26.5 %copy-start.5 = (bf16[128,768]{1,0:T(8,128)(2,1)}, bf16[128,768]{1,0:T(8,128)(2,1)S(1)}, u32[]{:S(2)}) copy-start(bf16[128,768]{1,0:T(8,128)(2,1)S(1)} %collective-permute-done.5.refs_4_) | copy-start | bytes 589828
  35.8 39.2 %collective-permute-start.7 = (bf16[128,768]{1,0:T(8,128)(2,1)}, bf16[128,768]{1,0:T(8,128)(2,1)S(1)}, u32[]{:S(2)}, u32[]{:S(2)}) collective-permute-start(bf16[128,768]{1,0:T(8,128)(2,1)} %get-tuple-element.23), channel_id=1, source_target_pairs={{0,4},{2,6},{4,0},{6,2},{1,5},{3,7},{5,1},{7,3},{8,12},{10,14},{12... | collective-permute-start | bytes 589832 | tf_op jit(solution)/shard_map/ppermute | solution.py:239
  52.7 9.7 %copy-start.8 = (bf16[96,1536]{1,0:T(8,128)(2,1)}, bf16[96,1536]{1,0:T(8,128)(2,1)S(1)}, u32[]{:S(2)}) copy-start(bf16[96,1536]{1,0:T(8,128)(2,1)S(1)} %collective-permute-done.10.refs_7_) | copy-start | bytes 884740
  52.7 24.5 %collective-permute-start.8 = (bf16[128,768]{1,0:T(8,128)(2,1)}, bf16[128,768]{1,0:T(8,128)(2,1)S(1)}, u32[]{:S(2)}, u32[]{:S(2)}) collective-permute-start(bf16[128,768]{1,0:T(8,128)(2,1)} %get-tuple-element.20), channel_id=1, source_target_pairs={{0,6},{2,4},{4,2},{6,0},{1,7},{3,5},{5,3},{7,1},{8,14},{10,12},{12... | collective-permute-start | bytes 589832 | tf_op jit(solution)/shard_map/ppermute | solution.py:239
  55.2 7.2 %copy-start.9 = (bf16[96,1536]{1,0:T(8,128)(2,1)}, bf16[96,1536]{1,0:T(8,128)(2,1)S(1)}, u32[]{:S(2)}) copy-start(bf16[96,1536]{1,0:T(8,128)(2,1)S(1)} %collective-permute-done.11.refs_8_) | copy-start | bytes 884740
  55.2 22.0 %collective-permute-start = (bf16[128,768]{1,0:T(8,128)(2,1)S(1)}, bf16[128,768]{1,0:T(8,128)(2,1)S(1)}, u32[]{:S(2)}, u32[]{:S(2)}) collective-permute-start(bf16[128,768]{1,0:T(8,128)(2,1)S(1)} %get-tuple-element.28), channel_id=1, source_target_pairs={{0,2},{2,0},{4,6},{6,4},{1,3},{3,1},{5,7},{7,5},{8,10},{10,8},{12,... | collective-permute-start | bytes 589832 | tf_op jit(solution)/shard_map/ppermute | solution.py:239
  62.3 0.7 copy-start.10
  72.7 45.7 %collective-permute-start.12 = (bf16[96,1536]{1,0:T(8,128)(2,1)}, bf16[96,1536]{1,0:T(8,128)(2,1)S(1)}, u32[]{:S(2)}, u32[]{:S(2)}) collective-permute-start(bf16[96,1536]{1,0:T(8,128)(2,1)} %get-tuple-element.13), channel_id=1, source_target_pairs={{2,0},{0,2},{6,4},{4,6},{3,1},{1,3},{7,5},{5,7},{10,8},{8,10},{14,... | collective-permute-start | bytes 884744 | tf_op jit(solution)/shard_map/ppermute | solution.py:248
  72.8 6.2 %copy-start.11 = (bf16[128,768]{1,0:T(8,128)(2,1)}, bf16[128,768]{1,0:T(8,128)(2,1)S(1)}, u32[]{:S(2)}) copy-start(bf16[128,768]{1,0:T(8,128)(2,1)S(1)} %collective-permute-done.6.refs_6_) | copy-start | bytes 589828
  72.8 45.6 %collective-permute-start.13 = (bf16[96,1536]{1,0:T(8,128)(2,1)}, bf16[96,1536]{1,0:T(8,128)(2,1)S(1)}, u32[]{:S(2)}, u32[]{:S(2)}) collective-permute-start(bf16[96,1536]{1,0:T(8,128)(2,1)} %get-tuple-element.14), channel_id=1, source_target_pairs={{4,0},{6,2},{0,4},{2,6},{5,1},{7,3},{1,5},{3,7},{12,8},{14,10},{8,... | collective-permute-start | bytes 884744 | tf_op jit(solution)/shard_map/ppermute | solution.py:248
  75.0 3.9 %copy-start.12 = (bf16[128,768]{1,0:T(8,128)(2,1)}, bf16[128,768]{1,0:T(8,128)(2,1)S(1)}, u32[]{:S(2)}) copy-start(bf16[128,768]{1,0:T(8,128)(2,1)S(1)} %collective-permute-done.7.refs_7_) | copy-start | bytes 589828
  75.0 45.0 %collective-permute-start.14 = (bf16[96,1536]{1,0:T(8,128)(2,1)}, bf16[96,1536]{1,0:T(8,128)(2,1)S(1)}, u32[]{:S(2)}, u32[]{:S(2)}) collective-permute-start(bf16[96,1536]{1,0:T(8,128)(2,1)} %get-tuple-element.15), channel_id=1, source_target_pairs={{6,0},{4,2},{2,4},{0,6},{7,1},{5,3},{3,5},{1,7},{14,8},{12,10},{10... | collective-permute-start | bytes 884744 | tf_op jit(solution)/shard_map/ppermute | solution.py:248
  77.2 1.8 %copy-start.14 = (bf16[128,768]{1,0:T(8,128)(2,1)}, bf16[128,768]{1,0:T(8,128)(2,1)S(1)}, u32[]{:S(2)}) copy-start(bf16[128,768]{1,0:T(8,128)(2,1)S(1)} %collective-permute-done.8.refs_8_) | copy-start | bytes 589828
  77.2 34.5 %collective-permute-start.1 = (bf16[128,768]{1,0:T(8,128)(2,1)S(1)}, bf16[128,768]{1,0:T(8,128)(2,1)S(1)}, u32[]{:S(2)}, u32[]{:S(2)}) collective-permute-start(bf16[128,768]{1,0:T(8,128)(2,1)S(1)} %get-tuple-element.30), channel_id=1, source_target_pairs={{0,4},{2,6},{4,0},{6,2},{1,5},{3,7},{5,1},{7,3},{8,12},{10,14},{12... | collective-permute-start | bytes 589832 | tf_op jit(solution)/shard_map/ppermute | solution.py:239
  77.2 8.7 %copy-start.13 = (bf16[128,768]{1,0:T(8,128)(2,1)}, bf16[128,768]{1,0:T(8,128)(2,1)S(1)}, u32[]{:S(2)}) copy-start(bf16[128,768]{1,0:T(8,128)(2,1)S(1)} %collective-permute-done.refs_1_) | copy-start | bytes 589828
  77.2 34.5 %collective-permute-start.2 = (bf16[128,768]{1,0:T(8,128)(2,1)S(1)}, bf16[128,768]{1,0:T(8,128)(2,1)S(1)}, u32[]{:S(2)}, u32[]{:S(2)}) collective-permute-start(bf16[128,768]{1,0:T(8,128)(2,1)S(1)} %get-tuple-element.27), channel_id=1, source_target_pairs={{0,6},{2,4},{4,2},{6,0},{1,7},{3,5},{5,3},{7,1},{8,14},{10,12},{12... | collective-permute-start | bytes 589832 | tf_op jit(solution)/shard_map/ppermute | solution.py:239
  111.6 0.7 copy-start.15
  111.7 0.7 copy-start.16
  112.4 6.0 %copy-start = (bf16[96,1536]{1,0:T(8,128)(2,1)S(1)}, bf16[96,1536]{1,0:T(8,128)(2,1)}, u32[]{:S(2)}) copy-start(bf16[96,1536]{1,0:T(8,128)(2,1)} %get-tuple-element.12.refs_1_) | copy-start | bytes 884740

commit v2 on v1

v2 whole, which is shorter than its diff:
```python
import jax
import jax.numpy as jnp
from jax import lax
from jax.experimental import pallas as pl
from jax.experimental.pallas import tpu as pltpu
from jax.sharding import PartitionSpec as P


HD = 128
GRANT = 24 << 20


def dot_nt(a, b):
    return lax.dot_general(a, b, (((1,), (1,)), ((), ())), preferred_element_type=jnp.float32)


def dot_nn(a, b):
    return lax.dot_general(a, b, (((1,), (0,)), ((), ())), preferred_element_type=jnp.float32)


def softmax_columns(scores):
    top = jnp.max(scores, axis=0, keepdims=True)
    weights = jnp.exp(scores - top)
    return weights / jnp.sum(weights, axis=0, keepdims=True)


def columns_of(ref, head, width):
    return ref[:, head * width : (head + 1) * width]


def stacked(refs, head, width):
    return jnp.concatenate([columns_of(ref, head, width) for ref in refs], axis=0)


def cross_kernel(count, origin, *refs):
    query_refs = refs[:count]
    text_refs = refs[count : 2 * count]
    grad_ref = refs[2 * count]
    out_ref = refs[2 * count + 1]
    piece_refs = refs[2 * count + 2 : 3 * count + 2]
    query_all = refs[3 * count + 2]
    scale = float(HD) ** (-0.5)
    here = lax.axis_index("head")
    rows = query_refs[0].shape[0]
    for at, ref in enumerate(query_refs):
        start = pl.multiple_of(origin(here, at) * rows, rows)
        query_all[pl.ds(start, rows), :] = ref[...]
    text_rows = text_refs[0].shape[0]
    for head in range(grad_ref.shape[1] // HD):
        query = columns_of(query_all, head, HD)
        grad = columns_of(grad_ref, head, HD)
        text = stacked(text_refs, head, 2 * HD)
        text_keys = text[:, :HD]
        text_values = text[:, HD:]
        probs = softmax_columns(dot_nt(text_keys, query) * scale)
        rounded = probs.astype(jnp.bfloat16)
        dprobs = dot_nt(text_values, grad)
        dscores = probs * (dprobs - jnp.sum(dprobs * probs, axis=0, keepdims=True))
        dscores = dscores.astype(jnp.bfloat16)
        grad_keys = (dot_nn(dscores, query) * scale).astype(jnp.bfloat16)
        grad_values = dot_nn(rounded, grad).astype(jnp.bfloat16)
        for at, ref in enumerate(piece_refs):
            part = slice(at * text_rows, (at + 1) * text_rows)
            ref[:, 2 * head * HD : (2 * head + 1) * HD] = grad_keys[part]
            ref[:, (2 * head + 1) * HD : (2 * head + 2) * HD] = grad_values[part]
        out_ref[:, head * HD : (head + 1) * HD] = dot_nn(text_values.T, rounded).T


def scores_kernel(count, origin, *refs):
    query_refs = refs[:count]
    key_refs = refs[count : 2 * count]
    probs_ref = refs[2 * count]
    scale = float(HD) ** (-0.5)
    here = lax.axis_index("head")
    rows, width = query_refs[0].shape
    length = rows * count
    for head in range(width // HD):
        keys = stacked(key_refs, head, HD)
        for at, ref in enumerate(query_refs):
            scores = dot_nt(columns_of(ref, head, HD), keys) * scale
            weights = jnp.exp(scores - jnp.max(scores, axis=1, keepdims=True))
            probs = weights / jnp.sum(weights, axis=1, keepdims=True)
            start = pl.multiple_of(origin(here, at) * rows, rows)
            probs_ref[pl.ds(start, rows), head * length : (head + 1) * length] = probs.astype(
                jnp.bfloat16
            )


def values_kernel(count, *refs):
    value_refs = refs[:count]
    probs_ref, cross_ref, out_ref = refs[count:]
    length, width = cross_ref.shape
    for head in range(width // HD):
        out = dot_nn(columns_of(probs_ref, head, length), stacked(value_refs, head, HD))
        out_ref[:, head * HD : (head + 1) * HD] = (out + columns_of(cross_ref, head, HD)).astype(
            jnp.bfloat16
        )


def vmem_call(kernel, out_shape, operands, scratch=()):
    many = isinstance(out_shape, list)
    spec = pl.BlockSpec(memory_space=pltpu.VMEM)
    return pl.pallas_call(
        kernel,
        out_shape=out_shape,
        in_specs=[spec] * len(operands),
        out_specs=[spec] * len(out_shape) if many else spec,
        scratch_shapes=list(scratch),
        compiler_params=pltpu.CompilerParams(vmem_limit_bytes=GRANT),
    )(*[pltpu.with_memory_space_constraint(operand, pltpu.VMEM) for operand in operands])


def cross_call(origin, query_pieces, text_pieces, cotangent):
    count = len(query_pieces)
    piece = pltpu.VMEM(text_pieces[0].shape, jnp.bfloat16)
    return vmem_call(
        lambda *refs: cross_kernel(count, origin, *refs),
        [pltpu.VMEM(cotangent.shape, jnp.float32)] + [piece] * count,
        [*query_pieces, *text_pieces, cotangent],
        [pltpu.VMEM(cotangent.shape, jnp.bfloat16)],
    )


def scores_call(origin, query_pieces, key_pieces):
    count = len(query_pieces)
    rows, width = query_pieces[0].shape
    length = rows * count
    return vmem_call(
        lambda *refs: scores_kernel(count, origin, *refs),
        pltpu.VMEM((length, (width // HD) * length), jnp.bfloat16),
        [*query_pieces, *key_pieces],
    )


def values_call(value_pieces, probs, cross_out):
    count = len(value_pieces)
    return vmem_call(
        lambda *refs: values_kernel(count, *refs),
        jax.ShapeDtypeStruct(cross_out.shape, jnp.bfloat16),
        [*value_pieces, probs, cross_out],
    )


def place_kernel(steps, order, *refs):
    pieces = refs[: len(steps)]
    out_ref, sems = refs[-2:]
    width = pieces[0].shape[1]
    copies = [
        pltpu.make_async_copy(
            piece,
            out_ref.at[:, pl.ds(pl.multiple_of(order[step] * width, width), width)],
            sems.at[at],
        )
        for at, (step, piece) in enumerate(zip(steps, pieces))
    ]
    for copy in copies:
        copy.start()
    for copy in copies:
        copy.wait()


def place_call(order, steps, pieces, whole=None):
    count = order.shape[0]
    rows, width = pieces[0].shape
    held = [] if whole is None else [whole]
    return pl.pallas_call(
        lambda *refs: place_kernel(steps, *refs),
        name="place",
        out_shape=jax.ShapeDtypeStruct((rows, width * count), pieces[0].dtype),
        in_specs=[pl.BlockSpec(memory_space=pltpu.SMEM)]
        + [pl.BlockSpec(memory_space=pltpu.VMEM)] * len(steps)
        + [pl.BlockSpec(memory_space=pl.ANY)] * len(held),
        out_specs=pl.BlockSpec(memory_space=pl.ANY),
        scratch_shapes=[pltpu.SemaphoreType.DMA((len(steps),))],
        input_output_aliases={len(steps) + 1: 0} if held else {},
        compiler_params=pltpu.CompilerParams(vmem_limit_bytes=GRANT),
    )(
        order,
        *[pltpu.with_memory_space_constraint(piece, pltpu.VMEM) for piece in pieces],
        *held,
    )


def pick_call(array, at, width):
    def pick_kernel(at, array_ref, out_ref, sem):
        start = pl.multiple_of(at[0] * width, width)
        copy = pltpu.make_async_copy(array_ref.at[:, pl.ds(start, width)], out_ref, sem)
        copy.start()
        copy.wait()

    return pl.pallas_call(
        pick_kernel,
        name="pick",
        out_shape=pltpu.VMEM((array.shape[0], width), array.dtype),
        in_specs=[pl.BlockSpec(memory_space=pltpu.SMEM), pl.BlockSpec(memory_space=pl.ANY)],
        out_specs=pl.BlockSpec(memory_space=pltpu.VMEM),
        scratch_shapes=[pltpu.SemaphoreType.DMA],
    )(at.reshape(1).astype(jnp.int32), array)


def send_order(count):
    near, far = [1], list(range(count - 1, 1, -1))
    first = [(name, step) for step in far[:1] for name in ("query", "text")]
    first += [(name, step) for step in near for name in ("query", "text", "key", "value")]
    later = [(name, step) for name in ("query", "text") for step in far[1:]]
    later += [(name, step) for name in ("key", "value") for step in far]
    return first + later


def solution(mesh):
    count = mesh.shape["head"]
    paired = count & (count - 1) == 0

    def target(index, step):
        return index ^ step if paired else (index + step) % count

    def origin(index, step):
        return index ^ step if paired else (index - step) % count

    def per_device(queries, keys, values, text_kv, cotangent):
        here = lax.axis_index("head")
        goal = jnp.stack([target(here, step) for step in range(count)]).astype(jnp.int32)
        arrays = {"query": queries[0], "text": text_kv[0], "key": keys[0], "value": values[0]}

        def columns(name, step):
            rows, width = arrays[name].shape
            width //= count
            at = target(here, step) * width
            return lax.dynamic_slice(arrays[name], (0, at), (rows, width))

        first, step = sends[0]
        held = pick_call(arrays[first], target(here, step), arrays[first].shape[1] // count)
        arrays[first], held = lax.optimization_barrier((arrays[first], held))
        got = {name: [columns(name, 0)] + [None] * (count - 1) for name in arrays}
        for at, (name, step) in enumerate(sends):
            got[name][step] = lax.ppermute(
                columns(name, step) if at else held,
                "head",
                [(index, target(index, step)) for index in range(count)],
            )
        cross_out, *grad_pieces = cross_call(origin, got["query"], got["text"], cotangent[0])
        back = [grad_pieces[0]]
        for step in range(1, count):
            back.append(
                lax.ppermute(
                    grad_pieces[step],
                    "head",
                    [(target(index, step), index) for index in range(count)],
                )
            )
        probs = scores_call(origin, got["query"], got["key"])
        attended = values_call(got["value"], probs, cross_out)
        text_grad = place_call(goal, tuple(range(count - 1)), back[:-1])
        last = back[-1]
        at = target(here, count - 1) * last.shape[1]
        text_grad = lax.dynamic_update_slice(text_grad, last, (0, at))
        return attended[None], text_grad[None]

    sends = send_order(count)

    placed = (
        P(("seq", "rep"), "head", None),
        P(("seq", "rep"), "head", None),
        P(("seq", "rep"), "head", None),
        P(("seq", "rep"), "head", None),
        P(("seq", "rep"), None, "head"),
    )
    return jax.shard_map(
        per_device,
        mesh=mesh,
        in_specs=placed,
        out_specs=(P(("seq", "rep"), None, "head"), P(("seq", "rep"), "head", None)),
        check_vma=False,
    )
```

time: 122 us -> 112 us (0.918); the launches traced: 121 us -> 112 us
  Pallas kernels: 25.2 us -> 11.8 us
  waiting for transfers between devices: 57.7 us -> 64.7 us
  local copies, waits for them, and re-layouts: 5.95 us -> 3.81 us
    pallas_call x3, Pallas kernels: 22.5 us -> 9.25 us  [vmem_call(): pl.pallas_call(kernel, out_shape=out_shape, in_specs=[spec] * len(operand...]
    ppermute x12, waiting for transfers between devices: 57.7 us -> 64.7 us  [per_device(): lax.ppermute(columns(name, step) if at else held, 'head', [(index, target...]
    unnamed x34 -> x8, local copies, waits for them, and re-layouts: 1.57 us -> 0.11 us
  transfers between devices with their start and end apart: 15 -> 15, of which waited for: 4 -> 4; matrix products, arithmetic and copies ran while one was open for 3% -> 2% of each run, Pallas kernels for 20% -> 10%
where the time goes in v2:
time: 112 us
  waiting for transfers between devices  64.7 us (58%)
  starting transfers between devices  30.9 us (28%)
  Pallas kernels  11.8 us (11%)
  local copies, waits for them, and re-layouts  3.81 us (3%)
    ppermute x12, waiting for transfers between devices, per_device(): lax.ppermute(columns(name, step) if at else held, 'head', [(index, target...  64.7 us
    ppermute x12, starting transfers between devices, per_device(): lax.ppermute(columns(name, step) if at else held, 'head', [(index, target...  26.5 us
    pallas_call x3, Pallas kernels, vmem_call(): pl.pallas_call(kernel, out_shape=out_shape, in_specs=[spec] * len(operand...  9.25 us
    ppermute x3, starting transfers between devices, per_device(): lax.ppermute(grad_pieces[step], 'head', [(target(index, step), index) for...  4.44 us
    dynamic_slice x4, local copies, waits for them, and re-layouts, columns(): return lax.dynamic_slice(arrays[name], (0, at), (rows, width))  2.96 us
  transfers between devices with their start and end apart: 15, of which 4 were waited for; matrix products, arithmetic and copies ran while one was open for 2% of the time, Pallas kernels for 10%

profile of v2, /device:TPU:0, one launch (start us, length us, event | category | flops | bytes accessed | tf_op | source)
XLA Modules:
  0.0 112.0 jit_solution(7606477412567402744)
XLA Ops:
  0.6 0.0 copy-start.1
  0.6 0.0 copy-start.2
  0.7 1.1 pick.1
  1.8 0.1 copy-done.1
  1.9 0.7 constant_dynamic-slice_fusion
  2.6 3.1 %collective-permute-start.3 = (bf16[128,768]{1,0:T(8,128)(2,1)}, bf16[128,768]{1,0:T(8,128)(2,1)S(1)}, u32[]{:S(2)}, u32[]{:S(2)}) collective-permute-start(bf16[128,768]{1,0:T(8,128)(2,1)} %get-tuple-element.25), channel_id=1, source_target_pairs={{0,2},{2,0},{4,6},{6,4},{1,3},{3,1},{5,7},{7,5},{8,10},{10,8},{12,... | collective-permute-start | bytes 589832 | tf_op jit(solution)/shard_map/ppermute | solution.py:236
  5.6 2.6 %collective-permute-start.4 = (bf16[128,768]{1,0:T(8,128)(2,1)S(1)}, bf16[128,768]{1,0:T(8,128)(2,1)S(1)}, u32[]{:S(2)}, u32[]{:S(2)}) collective-permute-start(bf16[128,768]{1,0:T(8,128)(2,1)S(1)} %get-tuple-element.24), channel_id=1, source_target_pairs={{0,4},{2,6},{4,0},{6,2},{1,5},{3,7},{5,1},{7,3},{8,12},{10,14},{12... | collective-permute-start | bytes 589832 | tf_op jit(solution)/shard_map/ppermute | solution.py:236
  8.2 0.0 collective-permute-start.5
  8.2 0.0 copy-done.2
  8.2 0.9 dynamic-slice_bitcast_fusion
  9.1 1.9 %collective-permute-start.10 = (bf16[96,1536]{1,0:T(8,128)(2,1)}, bf16[96,1536]{1,0:T(8,128)(2,1)S(1)}, u32[]{:S(2)}, u32[]{:S(2)}) collective-permute-start(bf16[96,1536]{1,0:T(8,128)(2,1)} %get-tuple-element.19), channel_id=1, source_target_pairs={{0,4},{2,6},{4,0},{6,2},{1,5},{3,7},{5,1},{7,3},{8,12},{10,14},{12... | collective-permute-start | bytes 884744 | tf_op jit(solution)/shard_map/ppermute | solution.py:236
  11.0 1.9 %collective-permute-start.11 = (bf16[96,1536]{1,0:T(8,128)(2,1)}, bf16[96,1536]{1,0:T(8,128)(2,1)S(1)}, u32[]{:S(2)}, u32[]{:S(2)}) collective-permute-start(bf16[96,1536]{1,0:T(8,128)(2,1)} %get-tuple-element.16), channel_id=1, source_target_pairs={{0,6},{2,4},{4,2},{6,0},{1,7},{3,5},{5,3},{7,1},{8,14},{10,12},{12... | collective-permute-start | bytes 884744 | tf_op jit(solution)/shard_map/ppermute | solution.py:236
  12.9 1.4 %collective-permute-done.3.refs_1_ = bf16[128,768]{1,0:T(8,128)(2,1)S(1)} collective-permute-done((bf16[128,768]{1,0:T(8,128)(2,1)}, bf16[128,768]{1,0:T(8,128)(2,1)S(1)}, u32[]{:S(2)}, u32[]{:S(2)}) %collective-permute-start.3) | collective-permute-done | bytes 196640 | tf_op jit(solution)/shard_map/ppermute | solution.py:236
  14.3 0.0 collective-permute-start.9
  14.3 1.3 %dynamic-slice_bitcast_fusion.4 = (bf16[128,768]{1,0:T(8,128)(2,1)S(1)}, bf16[128,768]{1,0:T(8,128)(2,1)S(1)}, bf16[128,768]{1,0:T(8,128)(2,1)S(1)}, bf16[128,768]{1,0:T(8,128)(2,1)S(1)}) fusion(bf16[1,128,3072]{2,1,0:T(8,128)(2,1)} %param.6, s32[]{:T(128)S(6)} %select_n.35, s32[]{:T(128)S(6)} %select_n.33, s32[]{:T(128)S(6)} %select_n.32, s32[]{:T(128)S(6)} %select_n.34), kind=kLoop, calls=%fused_computation.5 | loop fusion | bytes 1572880 | tf_op jit(solution)/shard_map/dynamic_slice | solution.py:229
  15.6 0.0 copy-start
  15.6 19.9 %collective-permute-done.4.refs_2_ = bf16[128,768]{1,0:T(8,128)(2,1)S(1)} collective-permute-done((bf16[128,768]{1,0:T(8,128)(2,1)S(1)}, bf16[128,768]{1,0:T(8,128)(2,1)S(1)}, u32[]{:S(2)}, u32[]{:S(2)}) %collective-permute-start.4) | collective-permute-done | bytes 196640 | tf_op jit(solution)/shard_map/ppermute | solution.py:236
  35.5 0.0 collective-permute-start.6
  35.5 0.0 collective-permute-done.5.refs_3_
  35.5 5.8 %collective-permute-start.7 = (bf16[128,768]{1,0:T(8,128)(2,1)S(1)}, bf16[128,768]{1,0:T(8,128)(2,1)S(1)}, u32[]{:S(2)}, u32[]{:S(2)}) collective-permute-start(bf16[128,768]{1,0:T(8,128)(2,1)S(1)} %get-tuple-element.23), channel_id=1, source_target_pairs={{0,4},{2,6},{4,0},{6,2},{1,5},{3,7},{5,1},{7,3},{8,12},{10,14},{12... | collective-permute-start | bytes 589832 | tf_op jit(solution)/shard_map/ppermute | solution.py:236
  41.2 0.0 copy-done.3
  41.2 0.1 dynamic-slice_bitcast_fusion.8
  41.3 11.0 %collective-permute-done.10.refs_6_ = bf16[96,1536]{1,0:T(8,128)(2,1)S(1)} collective-permute-done((bf16[96,1536]{1,0:T(8,128)(2,1)}, bf16[96,1536]{1,0:T(8,128)(2,1)S(1)}, u32[]{:S(2)}, u32[]{:S(2)}) %collective-permute-start.10) | collective-permute-done | bytes 294944 | tf_op jit(solution)/shard_map/ppermute | solution.py:236
  52.4 2.5 %collective-permute-start.8 = (bf16[128,768]{1,0:T(8,128)(2,1)S(1)}, bf16[128,768]{1,0:T(8,128)(2,1)S(1)}, u32[]{:S(2)}, u32[]{:S(2)}) collective-permute-start(bf16[128,768]{1,0:T(8,128)(2,1)S(1)} %get-tuple-element.20), channel_id=1, source_target_pairs={{0,6},{2,4},{4,2},{6,0},{1,7},{3,5},{5,3},{7,1},{8,14},{10,12},{12... | collective-permute-start | bytes 589832 | tf_op jit(solution)/shard_map/ppermute | solution.py:236
  54.8 0.0 collective-permute-done.11.refs_7_
  54.8 6.5 %collective-permute-start = (bf16[128,768]{1,0:T(8,128)(2,1)S(1)}, bf16[128,768]{1,0:T(8,128)(2,1)S(1)}, u32[]{:S(2)}, u32[]{:S(2)}) collective-permute-start(bf16[128,768]{1,0:T(8,128)(2,1)S(1)} %get-tuple-element.28), channel_id=1, source_target_pairs={{0,2},{2,0},{4,6},{6,4},{1,3},{3,1},{5,7},{7,5},{8,10},{10,8},{12,... | collective-permute-start | bytes 589832 | tf_op jit(solution)/shard_map/ppermute | solution.py:236
  61.3 0.0 collective-permute-done.9.refs_5_
  61.4 0.0 copy-done
  61.4 5.2 %shard_map.69 = (f32[512,768]{1,0:T(8,128)S(1)}, bf16[96,1536]{1,0:T(8,128)(2,1)S(1)}, bf16[96,1536]{1,0:T(8,128)(2,1)S(1)}, bf16[96,1536]{1,0:T(8,128)(2,1)S(1)}, bf16[96,1536]{1,0:T(8,128)(2,1)S(1)}) custom-call(bf16[128,768]{1,0:T(8,128)(2,1)S(1)} %get-tuple-element.26.refs_0_, bf16[128,768]{1,0:T(8,128)(2,1)S(1)} %collective-permute-done.3.refs_1_, ...), custom_call_target="tpu_custom_call" | custom-call | tf_op jit(solution)/shard_map/pallas_call | solution.py:103
  66.5 0.1 collective-permute-start.12
  66.6 0.0 collective-permute-done.6.refs_5_
  66.6 2.7 %collective-permute-start.13 = (bf16[96,1536]{1,0:T(8,128)(2,1)S(1)}, bf16[96,1536]{1,0:T(8,128)(2,1)S(1)}, u32[]{:S(2)}, u32[]{:S(2)}) collective-permute-start(bf16[96,1536]{1,0:T(8,128)(2,1)S(1)} %get-tuple-element.14), channel_id=1, source_target_pairs={{4,0},{6,2},{0,4},{2,6},{5,1},{7,3},{1,5},{3,7},{12,8},{14,10},{8,... | collective-permute-start | bytes 884744 | tf_op jit(solution)/shard_map/ppermute | solution.py:245
  69.3 0.0 collective-permute-done.7.refs_6_
  69.3 1.7 %collective-permute-start.14 = (bf16[96,1536]{1,0:T(8,128)(2,1)S(1)}, bf16[96,1536]{1,0:T(8,128)(2,1)S(1)}, u32[]{:S(2)}, u32[]{:S(2)}) collective-permute-start(bf16[96,1536]{1,0:T(8,128)(2,1)S(1)} %get-tuple-element.15), channel_id=1, source_target_pairs={{6,0},{4,2},{2,4},{0,6},{7,1},{5,3},{3,5},{1,7},{14,8},{12,10},{10... | collective-permute-start | bytes 884744 | tf_op jit(solution)/shard_map/ppermute | solution.py:245
  71.0 0.0 collective-permute-done.8.refs_7_
  71.0 0.4 collective-permute-start.1
  71.4 0.0 collective-permute-done.refs_1_
  71.4 1.9 %collective-permute-start.2 = (bf16[128,768]{1,0:T(8,128)(2,1)S(1)}, bf16[128,768]{1,0:T(8,128)(2,1)S(1)}, u32[]{:S(2)}, u32[]{:S(2)}) collective-permute-start(bf16[128,768]{1,0:T(8,128)(2,1)S(1)} %get-tuple-element.27), channel_id=1, source_target_pairs={{0,6},{2,4},{4,2},{6,0},{1,7},{3,5},{5,3},{7,1},{8,14},{10,12},{12... | collective-permute-start | bytes 589832 | tf_op jit(solution)/shard_map/ppermute | solution.py:236
  73.2 0.1 pad_add_fusion.refs_0_
  73.3 2.2 %shard_map.68.refs_4_ = bf16[512,3072]{1,0:T(8,128)(2,1)S(1)} custom-call(bf16[128,768]{1,0:T(8,128)(2,1)S(1)} %get-tuple-element.26.refs_0_, bf16[128,768]{1,0:T(8,128)(2,1)S(1)} %collective-permute-done.3.refs_1_, bf16[128,768]{1,0:T(8,128)(2,1)S(1)} %collective-permute-done.4.refs_2_, bf16[128,768]{1,0:T(8,128)(2,1)S(1)} %collective-permute-done.5.refs_3_, ...), custom_call_target="tpu_custom_call" | custom-call | tf_op jit(solution)/shard_map/pallas_call | solution.py:103
  75.5 32.4 %collective-permute-done.1.refs_2_ = bf16[128,768]{1,0:T(8,128)(2,1)S(1)} collective-permute-done((bf16[128,768]{1,0:T(8,128)(2,1)S(1)}, bf16[128,768]{1,0:T(8,128)(2,1)S(1)}, u32[]{:S(2)}, u32[]{:S(2)}) %collective-permute-start.1) | collective-permute-done | bytes 196640 | tf_op jit(solution)/shard_map/ppermute | solution.py:236
  107.9 0.0 collective-permute-done.2.refs_3_
  107.9 1.9 %shard_map.70 = bf16[512,768]{1,0:T(8,128)(2,1)} custom-call(bf16[128,768]{1,0:T(8,128)(2,1)S(1)} %get-tuple-element.29.refs_0_, bf16[128,768]{1,0:T(8,128)(2,1)S(1)} %collective-permute-done.refs_1_, bf16[128,768]{1,0:T(8,128)(2,1)S(1)} %collective-permute-done.1.refs_2_, bf16[128,768]{1,0:T(8,128)(2,1)S(1)} %collective-permute-done.2.refs_3_, ...), custom_call_target="tpu_custom_call" | custom-call | tf_op jit(solution)/shard_map/pallas_call | solution.py:103
  109.8 0.0 collective-permute-done.12.refs_2_
  109.8 0.0 collective-permute-done.13.refs_3_
  109.8 1.5 %place.1 = bf16[96,6144]{1,0:T(8,128)(2,1)} custom-call(s32[4]{0:T(128)S(1)} %pad_add_fusion.refs_0_, bf16[96,1536]{1,0:T(8,128)(2,1)S(1)} %get-tuple-element.12.refs_1_, bf16[96,1536]{1,0:T(8,128)(2,1)S(1)} %collective-permute-done.12.refs_2_, bf16[96,1536]{1,0:T(8,128)(2,1)S(1)} %collective-permute-done.13.refs_3_), custom_call_target="tpu_custom_call" | custom-call | tf_op jit(solution)/shard_map/place/pallas_call | solution.py:166
  111.3 0.0 collective-permute-done.14
  111.3 0.7 bitcast_dynamic-update-slice_fusion
  (1 shorter events, 0.0 us)
Async XLA Ops:
  0.6 1.2 %copy-start.1 = (bf16[1,128,3072]{2,1,0:T(8,128)(2,1)S(1)}, bf16[1,128,3072]{2,1,0:T(8,128)(2,1)}, u32[]{:S(2)}) copy-start(bf16[1,128,3072]{2,1,0:T(8,128)(2,1)} %param.5) | copy-start | bytes 2359300
  0.6 7.6 %copy-start.2 = (bf16[1,96,6144]{2,1,0:T(8,128)(2,1)S(1)}, bf16[1,96,6144]{2,1,0:T(8,128)(2,1)}, u32[]{:S(2)}) copy-start(bf16[1,96,6144]{2,1,0:T(8,128)(2,1)} %param.8) | copy-start | bytes 3538948
  2.6 11.7 %collective-permute-start.3 = (bf16[128,768]{1,0:T(8,128)(2,1)}, bf16[128,768]{1,0:T(8,128)(2,1)S(1)}, u32[]{:S(2)}, u32[]{:S(2)}) collective-permute-start(bf16[128,768]{1,0:T(8,128)(2,1)} %get-tuple-element.25), channel_id=1, source_target_pairs={{0,2},{2,0},{4,6},{6,4},{1,3},{3,1},{5,7},{7,5},{8,10},{10,8},{12,... | collective-permute-start | bytes 589832 | tf_op jit(solution)/shard_map/ppermute | solution.py:236
  5.6 29.8 %collective-permute-start.4 = (bf16[128,768]{1,0:T(8,128)(2,1)S(1)}, bf16[128,768]{1,0:T(8,128)(2,1)S(1)}, u32[]{:S(2)}, u32[]{:S(2)}) collective-permute-start(bf16[128,768]{1,0:T(8,128)(2,1)S(1)} %get-tuple-element.24), channel_id=1, source_target_pairs={{0,4},{2,6},{4,0},{6,2},{1,5},{3,7},{5,1},{7,3},{8,12},{10,14},{12... | collective-permute-start | bytes 589832 | tf_op jit(solution)/shard_map/ppermute | solution.py:236
  8.2 27.2 %collective-permute-start.5 = (bf16[128,768]{1,0:T(8,128)(2,1)S(1)}, bf16[128,768]{1,0:T(8,128)(2,1)S(1)}, u32[]{:S(2)}, u32[]{:S(2)}) collective-permute-start(bf16[128,768]{1,0:T(8,128)(2,1)S(1)} %pick.1), channel_id=1, source_target_pairs={{0,6},{2,4},{4,2},{6,0},{1,7},{3,5},{5,3},{7,1},{8,14},{10,12},{12... | collective-permute-start | bytes 589832 | tf_op jit(solution)/shard_map/ppermute | solution.py:236
  9.1 32.1 %copy-start.3 = (bf16[1,128,3072]{2,1,0:T(8,128)(2,1)S(1)}, bf16[1,128,3072]{2,1,0:T(8,128)(2,1)}, u32[]{:S(2)}) copy-start(bf16[1,128,3072]{2,1,0:T(8,128)(2,1)} %param.7) | copy-start | bytes 2359300
  9.1 43.2 %collective-permute-start.10 = (bf16[96,1536]{1,0:T(8,128)(2,1)}, bf16[96,1536]{1,0:T(8,128)(2,1)S(1)}, u32[]{:S(2)}, u32[]{:S(2)}) collective-permute-start(bf16[96,1536]{1,0:T(8,128)(2,1)} %get-tuple-element.19), channel_id=1, source_target_pairs={{0,4},{2,6},{4,0},{6,2},{1,5},{3,7},{5,1},{7,3},{8,12},{10,14},{12... | collective-permute-start | bytes 884744 | tf_op jit(solution)/shard_map/ppermute | solution.py:236
  11.0 43.8 %collective-permute-start.11 = (bf16[96,1536]{1,0:T(8,128)(2,1)}, bf16[96,1536]{1,0:T(8,128)(2,1)S(1)}, u32[]{:S(2)}, u32[]{:S(2)}) collective-permute-start(bf16[96,1536]{1,0:T(8,128)(2,1)} %get-tuple-element.16), channel_id=1, source_target_pairs={{0,6},{2,4},{4,2},{6,0},{1,7},{3,5},{5,3},{7,1},{8,14},{10,12},{12... | collective-permute-start | bytes 884744 | tf_op jit(solution)/shard_map/ppermute | solution.py:236
  14.3 47.0 %collective-permute-start.9 = (bf16[96,1536]{1,0:T(8,128)(2,1)S(1)}, bf16[96,1536]{1,0:T(8,128)(2,1)S(1)}, u32[]{:S(2)}, u32[]{:S(2)}) collective-permute-start(bf16[96,1536]{1,0:T(8,128)(2,1)S(1)} %get-tuple-element.17), channel_id=1, source_target_pairs={{0,2},{2,0},{4,6},{6,4},{1,3},{3,1},{5,7},{7,5},{8,10},{10,8},{12,... | collective-permute-start | bytes 884744 | tf_op jit(solution)/shard_map/ppermute | solution.py:236
  15.6 45.8 %copy-start = (bf16[1,512,768]{2,1,0:T(8,128)(2,1)S(1)}, bf16[1,512,768]{2,1,0:T(8,128)(2,1)}, u32[]{:S(2)}) copy-start(bf16[1,512,768]{2,1,0:T(8,128)(2,1)} %param.9) | copy-start | bytes 2359300
  35.5 31.2 %collective-permute-start.6 = (bf16[128,768]{1,0:T(8,128)(2,1)S(1)}, bf16[128,768]{1,0:T(8,128)(2,1)S(1)}, u32[]{:S(2)}, u32[]{:S(2)}) collective-permute-start(bf16[128,768]{1,0:T(8,128)(2,1)S(1)} %get-tuple-element.21), channel_id=1, source_target_pairs={{0,2},{2,0},{4,6},{6,4},{1,3},{3,1},{5,7},{7,5},{8,10},{10,8},{12,... | collective-permute-start | bytes 589832 | tf_op jit(solution)/shard_map/ppermute | solution.py:236
  35.5 33.9 %collective-permute-start.7 = (bf16[128,768]{1,0:T(8,128)(2,1)S(1)}, bf16[128,768]{1,0:T(8,128)(2,1)S(1)}, u32[]{:S(2)}, u32[]{:S(2)}) collective-permute-start(bf16[128,768]{1,0:T(8,128)(2,1)S(1)} %get-tuple-element.23), channel_id=1, source_target_pairs={{0,4},{2,6},{4,0},{6,2},{1,5},{3,7},{5,1},{7,3},{8,12},{10,14},{12... | collective-permute-start | bytes 589832 | tf_op jit(solution)/shard_map/ppermute | solution.py:236
  52.4 18.6 %collective-permute-start.8 = (bf16[128,768]{1,0:T(8,128)(2,1)S(1)}, bf16[128,768]{1,0:T(8,128)(2,1)S(1)}, u32[]{:S(2)}, u32[]{:S(2)}) collective-permute-start(bf16[128,768]{1,0:T(8,128)(2,1)S(1)} %get-tuple-element.20), channel_id=1, source_target_pairs={{0,6},{2,4},{4,2},{6,0},{1,7},{3,5},{5,3},{7,1},{8,14},{10,12},{12... | collective-permute-start | bytes 589832 | tf_op jit(solution)/shard_map/ppermute | solution.py:236
  54.8 16.5 %collective-permute-start = (bf16[128,768]{1,0:T(8,128)(2,1)S(1)}, bf16[128,768]{1,0:T(8,128)(2,1)S(1)}, u32[]{:S(2)}, u32[]{:S(2)}) collective-permute-start(bf16[128,768]{1,0:T(8,128)(2,1)S(1)} %get-tuple-element.28), channel_id=1, source_target_pairs={{0,2},{2,0},{4,6},{6,4},{1,3},{3,1},{5,7},{7,5},{8,10},{10,8},{12,... | collective-permute-start | bytes 589832 | tf_op jit(solution)/shard_map/ppermute | solution.py:236
  66.5 43.2 %collective-permute-start.12 = (bf16[96,1536]{1,0:T(8,128)(2,1)S(1)}, bf16[96,1536]{1,0:T(8,128)(2,1)S(1)}, u32[]{:S(2)}, u32[]{:S(2)}) collective-permute-start(bf16[96,1536]{1,0:T(8,128)(2,1)S(1)} %get-tuple-element.13), channel_id=1, source_target_pairs={{2,0},{0,2},{6,4},{4,6},{3,1},{1,3},{7,5},{5,7},{10,8},{8,10},{14,... | collective-permute-start | bytes 884744 | tf_op jit(solution)/shard_map/ppermute | solution.py:245
  66.6 43.2 %collective-permute-start.13 = (bf16[96,1536]{1,0:T(8,128)(2,1)S(1)}, bf16[96,1536]{1,0:T(8,128)(2,1)S(1)}, u32[]{:S(2)}, u32[]{:S(2)}) collective-permute-start(bf16[96,1536]{1,0:T(8,128)(2,1)S(1)} %get-tuple-element.14), channel_id=1, source_target_pairs={{4,0},{6,2},{0,4},{2,6},{5,1},{7,3},{1,5},{3,7},{12,8},{14,10},{8,... | collective-permute-start | bytes 884744 | tf_op jit(solution)/shard_map/ppermute | solution.py:245
  69.3 42.0 %collective-permute-start.14 = (bf16[96,1536]{1,0:T(8,128)(2,1)S(1)}, bf16[96,1536]{1,0:T(8,128)(2,1)S(1)}, u32[]{:S(2)}, u32[]{:S(2)}) collective-permute-start(bf16[96,1536]{1,0:T(8,128)(2,1)S(1)} %get-tuple-element.15), channel_id=1, source_target_pairs={{6,0},{4,2},{2,4},{0,6},{7,1},{5,3},{3,5},{1,7},{14,8},{12,10},{10... | collective-permute-start | bytes 884744 | tf_op jit(solution)/shard_map/ppermute | solution.py:245
  71.0 36.9 %collective-permute-start.1 = (bf16[128,768]{1,0:T(8,128)(2,1)S(1)}, bf16[128,768]{1,0:T(8,128)(2,1)S(1)}, u32[]{:S(2)}, u32[]{:S(2)}) collective-permute-start(bf16[128,768]{1,0:T(8,128)(2,1)S(1)} %get-tuple-element.30), channel_id=1, source_target_pairs={{0,4},{2,6},{4,0},{6,2},{1,5},{3,7},{5,1},{7,3},{8,12},{10,14},{12... | collective-permute-start | bytes 589832 | tf_op jit(solution)/shard_map/ppermute | solution.py:236
  71.4 36.5 %collective-permute-start.2 = (bf16[128,768]{1,0:T(8,128)(2,1)S(1)}, bf16[128,768]{1,0:T(8,128)(2,1)S(1)}, u32[]{:S(2)}, u32[]{:S(2)}) collective-permute-start(bf16[128,768]{1,0:T(8,128)(2,1)S(1)} %get-tuple-element.27), channel_id=1, source_target_pairs={{0,6},{2,4},{4,2},{6,0},{1,7},{3,5},{5,3},{7,1},{8,14},{10,12},{12... | collective-permute-start | bytes 589832 | tf_op jit(solution)/shard_map/ppermute | solution.py:236

commit v3 on v2

--- a/solution.py
+++ b/solution.py
@@ -37,8 +37,8 @@
     text_refs = refs[count : 2 * count]
     grad_ref = refs[2 * count]
     out_ref = refs[2 * count + 1]
-    piece_refs = refs[2 * count + 2 : 3 * count + 2]
-    query_all = refs[3 * count + 2]
+    piece_refs = refs[2 * count + 2 : 3 * count + 1]
+    rest_ref, most_ref, query_all = refs[3 * count + 1 :]
     scale = float(HD) ** (-0.5)
     here = lax.axis_index("head")
     rows = query_refs[0].shape[0]
@@ -59,10 +59,15 @@
         dscores = dscores.astype(jnp.bfloat16)
         grad_keys = (dot_nn(dscores, query) * scale).astype(jnp.bfloat16)
         grad_values = dot_nn(rounded, grad).astype(jnp.bfloat16)
-        for at, ref in enumerate(piece_refs):
+        places = [(ref, 2 * head * HD) for ref in piece_refs]
+        few = rest_ref.shape[1] // (2 * HD)
+        places.append(
+            (rest_ref, 2 * head * HD) if head < few else (most_ref, 2 * (head - few) * HD)
+        )
+        for at, (ref, start) in enumerate(places):
             part = slice(at * text_rows, (at + 1) * text_rows)
-            ref[:, 2 * head * HD : (2 * head + 1) * HD] = grad_keys[part]
-            ref[:, (2 * head + 1) * HD : (2 * head + 2) * HD] = grad_values[part]
+            ref[:, start : start + HD] = grad_keys[part]
+            ref[:, start + HD : start + 2 * HD] = grad_values[part]
         out_ref[:, head * HD : (head + 1) * HD] = dot_nn(text_values.T, rounded).T
 
 
@@ -112,10 +117,12 @@
 
 def cross_call(origin, query_pieces, text_pieces, cotangent):
     count = len(query_pieces)
-    piece = pltpu.VMEM(text_pieces[0].shape, jnp.bfloat16)
+    rows, width = text_pieces[0].shape
+    pieces = [pltpu.VMEM((rows, width), jnp.bfloat16)] * (count - 1)
+    pieces += [pltpu.VMEM((rows, wide), jnp.bfloat16) for wide in (width // 2, width // 2)]
     return vmem_call(
         lambda *refs: cross_kernel(count, origin, *refs),
-        [pltpu.VMEM(cotangent.shape, jnp.float32)] + [piece] * count,
+        [pltpu.VMEM(cotangent.shape, jnp.float32)] + pieces,
         [*query_pieces, *text_pieces, cotangent],
         [pltpu.VMEM(cotangent.shape, jnp.bfloat16)],
     )
@@ -145,14 +152,11 @@
     pieces = refs[: len(steps)]
     out_ref, sems = refs[-2:]
     width = pieces[0].shape[1]
-    copies = [
-        pltpu.make_async_copy(
-            piece,
-            out_ref.at[:, pl.ds(pl.multiple_of(order[step] * width, width), width)],
-            sems.at[at],
-        )
-        for at, (step, piece) in enumerate(zip(steps, pieces))
-    ]
+    copies = []
+    for at, (step, piece) in enumerate(zip(steps, pieces)):
+        start = pl.multiple_of(order[step] * width, width) + width - piece.shape[1]
+        spot = out_ref.at[:, pl.ds(pl.multiple_of(start, HD), piece.shape[1])]
+        copies.append(pltpu.make_async_copy(piece, spot, sems.at[at]))
     for copy in copies:
         copy.start()
     for copy in copies:
@@ -239,21 +243,22 @@
                 [(index, target(index, step)) for index in range(count)],
             )
         cross_out, *grad_pieces = cross_call(origin, got["query"], got["text"], cotangent[0])
+
+        def send_back(piece, step):
+            return lax.ppermute(
+                piece, "head", [(target(index, step), index) for index in range(count)]
+            )
+
         back = [grad_pieces[0]]
-        for step in range(1, count):
-            back.append(
-                lax.ppermute(
-                    grad_pieces[step],
-                    "head",
-                    [(target(index, step), index) for index in range(count)],
-                )
-            )
+        for step in range(1, count - 1):
+            back.append(send_back(grad_pieces[step], step))
+        most = send_back(grad_pieces[count], count - 1)
+        rest = send_back(grad_pieces[count - 1], count - 1)
         probs = scores_call(origin, got["query"], got["key"])
         attended = values_call(got["value"], probs, cross_out)
-        text_grad = place_call(goal, tuple(range(count - 1)), back[:-1])
-        last = back[-1]
-        at = target(here, count - 1) * last.shape[1]
-        text_grad = lax.dynamic_update_slice(text_grad, last, (0, at))
+        text_grad = place_call(goal, tuple(range(count)), back + [most])
+        at = target(here, count - 1) * grad_pieces[0].shape[1]
+        text_grad = lax.dynamic_update_slice(text_grad, rest, (0, at))
         return attended[None], text_grad[None]
 
     sends = send_order(count)

time: 112 us -> 109 us (0.973)
  the two profiles are of different devices: /device:TPU:0 before, /device:TPU:10 now
where the time goes in v3:
time: 109 us
  waiting for transfers between devices  71.2 us (65%)
  starting transfers between devices  20.4 us (19%)
  Pallas kernels  11.8 us (11%)
  local copies, waits for them, and re-layouts  4.84 us (4%)
    ppermute x12, waiting for transfers between devices, per_device(): lax.ppermute(columns(name, step) if at else held, 'head', [(index, target...  69.7 us
    ppermute x12, starting transfers between devices, per_device(): lax.ppermute(columns(name, step) if at else held, 'head', [(index, target...  17.5 us
    pallas_call x3, Pallas kernels, vmem_call(): pl.pallas_call(kernel, out_shape=out_shape, in_specs=[spec] * len(operand...  9.24 us
    dynamic_slice x4, local copies, waits for them, and re-layouts, columns(): return lax.dynamic_slice(arrays[name], (0, at), (rows, width))  4.06 us
    ppermute x4, starting transfers between devices, send_back(): lax.ppermute(piece, 'head', [(target(index, step), index) for index in ra...  2.9 us
  transfers between devices with their start and end apart: 16, of which 9 were waited for; matrix products, arithmetic and copies ran while one was open for 3% of the time, Pallas kernels for 10%

profile of v3, /device:TPU:10, one launch (start us, length us, event | category | flops | bytes accessed | tf_op | source)
XLA Modules:
  0.0 109.1 jit_solution(9687215233894512425)
XLA Ops:
  0.6 0.0 copy-start.1
  0.6 0.0 copy-start.2
  0.7 1.1 pick.1
  1.8 0.1 copy-done.1
  1.9 0.7 constant_dynamic-slice_fusion
  2.6 0.4 collective-permute-start.3
  3.0 0.0 copy-done.2
  3.0 0.8 dynamic-slice_bitcast_fusion
  3.8 2.6 %collective-permute-start.10 = (bf16[96,1536]{1,0:T(8,128)(2,1)}, bf16[96,1536]{1,0:T(8,128)(2,1)S(1)}, u32[]{:S(2)}, u32[]{:S(2)}) collective-permute-start(bf16[96,1536]{1,0:T(8,128)(2,1)} %get-tuple-element.21), channel_id=1, source_target_pairs={{0,4},{2,6},{4,0},{6,2},{1,5},{3,7},{5,1},{7,3},{8,12},{10,14},{12... | collective-permute-start | bytes 884744 | tf_op jit(solution)/shard_map/ppermute | solution.py:240
  6.4 0.3 collective-permute-start.4
  6.8 2.7 %collective-permute-start.5 = (bf16[128,768]{1,0:T(8,128)(2,1)S(1)}, bf16[128,768]{1,0:T(8,128)(2,1)S(1)}, u32[]{:S(2)}, u32[]{:S(2)}) collective-permute-start(bf16[128,768]{1,0:T(8,128)(2,1)S(1)} %pick.1), channel_id=1, source_target_pairs={{0,6},{2,4},{4,2},{6,0},{1,7},{3,5},{5,3},{7,1},{8,14},{10,12},{12... | collective-permute-start | bytes 589832 | tf_op jit(solution)/shard_map/ppermute | solution.py:240
  9.5 0.0 collective-permute-start.11
  9.5 0.6 collective-permute-done.3.refs_1_
  10.1 2.4 %collective-permute-start.9 = (bf16[96,1536]{1,0:T(8,128)(2,1)S(1)}, bf16[96,1536]{1,0:T(8,128)(2,1)S(1)}, u32[]{:S(2)}, u32[]{:S(2)}) collective-permute-start(bf16[96,1536]{1,0:T(8,128)(2,1)S(1)} %get-tuple-element.19), channel_id=1, source_target_pairs={{0,2},{2,0},{4,6},{6,4},{1,3},{3,1},{5,7},{7,5},{8,10},{10,8},{12,... | collective-permute-start | bytes 884744 | tf_op jit(solution)/shard_map/ppermute | solution.py:240
  12.5 1.3 %dynamic-slice_bitcast_fusion.4 = (bf16[128,768]{1,0:T(8,128)(2,1)S(1)}, bf16[128,768]{1,0:T(8,128)(2,1)S(1)}, bf16[128,768]{1,0:T(8,128)(2,1)S(1)}, bf16[128,768]{1,0:T(8,128)(2,1)S(1)}) fusion(bf16[1,128,3072]{2,1,0:T(8,128)(2,1)} %param.6, s32[]{:T(128)S(6)} %select_n.35, s32[]{:T(128)S(6)} %select_n.33, s32[]{:T(128)S(6)} %select_n.32, s32[]{:T(128)S(6)} %select_n.34), kind=kLoop, calls=%fused_computation.4 | loop fusion | bytes 1572880 | tf_op jit(solution)/shard_map/dynamic_slice | solution.py:233
  13.8 0.0 copy-start
  13.8 25.4 %collective-permute-done.4.refs_2_ = bf16[128,768]{1,0:T(8,128)(2,1)S(1)} collective-permute-done((bf16[128,768]{1,0:T(8,128)(2,1)}, bf16[128,768]{1,0:T(8,128)(2,1)S(1)}, u32[]{:S(2)}, u32[]{:S(2)}) %collective-permute-start.4) | collective-permute-done | bytes 196640 | tf_op jit(solution)/shard_map/ppermute | solution.py:240
  39.2 2.5 %collective-permute-start.6 = (bf16[128,768]{1,0:T(8,128)(2,1)S(1)}, bf16[128,768]{1,0:T(8,128)(2,1)S(1)}, u32[]{:S(2)}, u32[]{:S(2)}) collective-permute-start(bf16[128,768]{1,0:T(8,128)(2,1)S(1)} %get-tuple-element.23), channel_id=1, source_target_pairs={{0,2},{2,0},{4,6},{6,4},{1,3},{3,1},{5,7},{7,5},{8,10},{10,8},{12,... | collective-permute-start | bytes 589832 | tf_op jit(solution)/shard_map/ppermute | solution.py:240
  41.7 2.7 %collective-permute-done.5.refs_3_ = bf16[128,768]{1,0:T(8,128)(2,1)S(1)} collective-permute-done((bf16[128,768]{1,0:T(8,128)(2,1)S(1)}, bf16[128,768]{1,0:T(8,128)(2,1)S(1)}, u32[]{:S(2)}, u32[]{:S(2)}) %collective-permute-start.5) | collective-permute-done | bytes 196640 | tf_op jit(solution)/shard_map/ppermute | solution.py:240
  44.4 0.0 collective-permute-start.7
  44.4 0.0 collective-permute-done.10.refs_6_
  44.4 1.4 %collective-permute-start.8 = (bf16[128,768]{1,0:T(8,128)(2,1)S(1)}, bf16[128,768]{1,0:T(8,128)(2,1)S(1)}, u32[]{:S(2)}, u32[]{:S(2)}) collective-permute-start(bf16[128,768]{1,0:T(8,128)(2,1)S(1)} %get-tuple-element.22), channel_id=1, source_target_pairs={{0,6},{2,4},{4,2},{6,0},{1,7},{3,5},{5,3},{7,1},{8,14},{10,12},{12... | collective-permute-start | bytes 589832 | tf_op jit(solution)/shard_map/ppermute | solution.py:240
  45.8 1.3 %dynamic-slice_bitcast_fusion.8 = (bf16[128,768]{1,0:T(8,128)(2,1)S(1)}, bf16[128,768]{1,0:T(8,128)(2,1)S(1)}, bf16[128,768]{1,0:T(8,128)(2,1)S(1)}, bf16[128,768]{1,0:T(8,128)(2,1)S(1)}) fusion(bf16[1,128,3072]{2,1,0:T(8,128)(2,1)} %param.7, s32[]{:T(128)S(6)} %select_n.35, s32[]{:T(128)S(6)} %select_n.33, s32[]{:T(128)S(6)} %select_n.32, s32[]{:T(128)S(6)} %select_n.34), kind=kLoop, calls=%fused_computation.8 | loop fusion | bytes 1572880 | tf_op jit(solution)/shard_map/dynamic_slice | solution.py:233
  47.1 12.1 %collective-permute-done.11.refs_7_ = bf16[96,1536]{1,0:T(8,128)(2,1)S(1)} collective-permute-done((bf16[96,1536]{1,0:T(8,128)(2,1)S(1)}, bf16[96,1536]{1,0:T(8,128)(2,1)S(1)}, u32[]{:S(2)}, u32[]{:S(2)}) %collective-permute-start.11) | collective-permute-done | bytes 294944 | tf_op jit(solution)/shard_map/ppermute | solution.py:240
  59.2 0.0 collective-permute-start
  59.2 0.0 collective-permute-done.9.refs_5_
  59.2 2.8 %collective-permute-start.1 = (bf16[128,768]{1,0:T(8,128)(2,1)S(1)}, bf16[128,768]{1,0:T(8,128)(2,1)S(1)}, u32[]{:S(2)}, u32[]{:S(2)}) collective-permute-start(bf16[128,768]{1,0:T(8,128)(2,1)S(1)} %get-tuple-element.32), channel_id=1, source_target_pairs={{0,4},{2,6},{4,0},{6,2},{1,5},{3,7},{5,1},{7,3},{8,12},{10,14},{12... | collective-permute-start | bytes 589832 | tf_op jit(solution)/shard_map/ppermute | solution.py:240
  62.0 5.2 %shard_map.69 = (f32[512,768]{1,0:T(8,128)S(1)}, bf16[96,1536]{1,0:T(8,128)(2,1)S(1)}, bf16[96,1536]{1,0:T(8,128)(2,1)S(1)}, bf16[96,1536]{1,0:T(8,128)(2,1)S(1)...) custom-call(bf16[128,768]{1,0:T(8,128)(2,1)S(1)} %get-tuple-element.28.refs_0_, ...), custom_call_target="tpu_custom_call" | custom-call | tf_op jit(solution)/shard_map/pallas_call | solution.py:108
  67.2 0.0 collective-permute-done.6.refs_5_
  67.2 0.1 collective-permute-start.12
  67.3 0.0 collective-permute-done.7.refs_6_
  67.3 2.1 %collective-permute-start.13 = (bf16[96,1536]{1,0:T(8,128)(2,1)S(1)}, bf16[96,1536]{1,0:T(8,128)(2,1)S(1)}, u32[]{:S(2)}, u32[]{:S(2)}) collective-permute-start(bf16[96,1536]{1,0:T(8,128)(2,1)S(1)} %get-tuple-element.15), channel_id=1, source_target_pairs={{4,0},{6,2},{0,4},{2,6},{5,1},{7,3},{1,5},{3,7},{12,8},{14,10},{8,... | collective-permute-start | bytes 884744 | tf_op jit(solution)/shard_map/ppermute | solution.py:248
  69.4 2.5 %collective-permute-done.8.refs_7_ = bf16[128,768]{1,0:T(8,128)(2,1)S(1)} collective-permute-done((bf16[128,768]{1,0:T(8,128)(2,1)S(1)}, bf16[128,768]{1,0:T(8,128)(2,1)S(1)}, u32[]{:S(2)}, u32[]{:S(2)}) %collective-permute-start.8) | collective-permute-done | bytes 196640 | tf_op jit(solution)/shard_map/ppermute | solution.py:240
  71.9 2.3 %collective-permute-start.2 = (bf16[128,768]{1,0:T(8,128)(2,1)S(1)}, bf16[128,768]{1,0:T(8,128)(2,1)S(1)}, u32[]{:S(2)}, u32[]{:S(2)}) collective-permute-start(bf16[128,768]{1,0:T(8,128)(2,1)S(1)} %get-tuple-element.29), channel_id=1, source_target_pairs={{0,6},{2,4},{4,2},{6,0},{1,7},{3,5},{5,3},{7,1},{8,14},{10,12},{12... | collective-permute-start | bytes 589832 | tf_op jit(solution)/shard_map/ppermute | solution.py:240
  74.2 0.0 collective-permute-done.refs_1_
  74.2 0.0 collective-permute-start.14
  74.2 16.0 %collective-permute-done.1.refs_2_ = bf16[128,768]{1,0:T(8,128)(2,1)S(1)} collective-permute-done((bf16[128,768]{1,0:T(8,128)(2,1)S(1)}, bf16[128,768]{1,0:T(8,128)(2,1)S(1)}, u32[]{:S(2)}, u32[]{:S(2)}) %collective-permute-start.1) | collective-permute-done | bytes 196640 | tf_op jit(solution)/shard_map/ppermute | solution.py:240
  90.2 0.7 collective-permute-start.15
  90.9 0.1 pad_add_fusion.refs_0_
  91.0 2.2 %shard_map.68.refs_4_ = bf16[512,3072]{1,0:T(8,128)(2,1)S(1)} custom-call(bf16[128,768]{1,0:T(8,128)(2,1)S(1)} %get-tuple-element.28.refs_0_, bf16[128,768]{1,0:T(8,128)(2,1)S(1)} %collective-permute-done.3.refs_1_, bf16[128,768]{1,0:T(8,128)(2,1)S(1)} %collective-permute-done.4.refs_2_, bf16[128,768]{1,0:T(8,128)(2,1)S(1)} %collective-permute-done.5.refs_3_, ...), custom_call_target="tpu_custom_call" | custom-call | tf_op jit(solution)/shard_map/pallas_call | solution.py:108
  93.2 10.3 %collective-permute-done.2.refs_3_ = bf16[128,768]{1,0:T(8,128)(2,1)S(1)} collective-permute-done((bf16[128,768]{1,0:T(8,128)(2,1)S(1)}, bf16[128,768]{1,0:T(8,128)(2,1)S(1)}, u32[]{:S(2)}, u32[]{:S(2)}) %collective-permute-start.2) | collective-permute-done | bytes 196640 | tf_op jit(solution)/shard_map/ppermute | solution.py:240
  103.5 1.9 %shard_map.70 = bf16[512,768]{1,0:T(8,128)(2,1)} custom-call(bf16[128,768]{1,0:T(8,128)(2,1)S(1)} %get-tuple-element.31.refs_0_, bf16[128,768]{1,0:T(8,128)(2,1)S(1)} %collective-permute-done.refs_1_, bf16[128,768]{1,0:T(8,128)(2,1)S(1)} %collective-permute-done.1.refs_2_, bf16[128,768]{1,0:T(8,128)(2,1)S(1)} %collective-permute-done.2.refs_3_, ...), custom_call_target="tpu_custom_call" | custom-call | tf_op jit(solution)/shard_map/pallas_call | solution.py:108
  105.4 1.3 %collective-permute-done.14.refs_4_ = bf16[96,768]{1,0:T(8,128)(2,1)S(1)} collective-permute-done((bf16[96,768]{1,0:T(8,128)(2,1)S(1)}, bf16[96,768]{1,0:T(8,128)(2,1)S(1)}, u32[]{:S(2)}, u32[]{:S(2)}) %collective-permute-start.14) | collective-permute-done | bytes 147488 | tf_op jit(solution)/shard_map/ppermute | solution.py:248
  106.7 0.0 collective-permute-done.12.refs_2_
  106.7 0.0 collective-permute-done.13.refs_3_
  106.7 1.5 %place.1 = bf16[96,6144]{1,0:T(8,128)(2,1)} custom-call(s32[4]{0:T(128)S(1)} %pad_add_fusion.refs_0_, bf16[96,1536]{1,0:T(8,128)(2,1)S(1)} %get-tuple-element.13.refs_1_, bf16[96,1536]{1,0:T(8,128)(2,1)S(1)} %collective-permute-done.12.refs_2_, bf16[96,1536]{1,0:T(8,128)(2,1)S(1)} %collective-permute-done.13.refs_3_, ...), custom_call_target="tpu_custom_call" | custom-call | tf_op jit(solution)/shard_map/place/pallas_call | solution.py:170
  108.2 0.2 collective-permute-done.15
  108.5 0.7 bitcast_dynamic-update-slice_fusion
  (1 shorter events, 0.0 us)
Async XLA Ops:
  0.6 1.2 %copy-start.1 = (bf16[1,128,3072]{2,1,0:T(8,128)(2,1)S(1)}, bf16[1,128,3072]{2,1,0:T(8,128)(2,1)}, u32[]{:S(2)}) copy-start(bf16[1,128,3072]{2,1,0:T(8,128)(2,1)} %param.5) | copy-start | bytes 2359300
  0.6 2.4 %copy-start.2 = (bf16[1,96,6144]{2,1,0:T(8,128)(2,1)S(1)}, bf16[1,96,6144]{2,1,0:T(8,128)(2,1)}, u32[]{:S(2)}) copy-start(bf16[1,96,6144]{2,1,0:T(8,128)(2,1)} %param.8) | copy-start | bytes 3538948
  2.6 7.5 %collective-permute-start.3 = (bf16[128,768]{1,0:T(8,128)(2,1)S(1)}, bf16[128,768]{1,0:T(8,128)(2,1)S(1)}, u32[]{:S(2)}, u32[]{:S(2)}) collective-permute-start(bf16[128,768]{1,0:T(8,128)(2,1)S(1)} %get-tuple-element.27), channel_id=1, source_target_pairs={{0,2},{2,0},{4,6},{6,4},{1,3},{3,1},{5,7},{7,5},{8,10},{10,8},{12,... | collective-permute-start | bytes 589832 | tf_op jit(solution)/shard_map/ppermute | solution.py:240
  3.8 40.6 %collective-permute-start.10 = (bf16[96,1536]{1,0:T(8,128)(2,1)}, bf16[96,1536]{1,0:T(8,128)(2,1)S(1)}, u32[]{:S(2)}, u32[]{:S(2)}) collective-permute-start(bf16[96,1536]{1,0:T(8,128)(2,1)} %get-tuple-element.21), channel_id=1, source_target_pairs={{0,4},{2,6},{4,0},{6,2},{1,5},{3,7},{5,1},{7,3},{8,12},{10,14},{12... | collective-permute-start | bytes 884744 | tf_op jit(solution)/shard_map/ppermute | solution.py:240
  6.4 32.8 %collective-permute-start.4 = (bf16[128,768]{1,0:T(8,128)(2,1)}, bf16[128,768]{1,0:T(8,128)(2,1)S(1)}, u32[]{:S(2)}, u32[]{:S(2)}) collective-permute-start(bf16[128,768]{1,0:T(8,128)(2,1)} %get-tuple-element.26), channel_id=1, source_target_pairs={{0,4},{2,6},{4,0},{6,2},{1,5},{3,7},{5,1},{7,3},{8,12},{10,14},{12... | collective-permute-start | bytes 589832 | tf_op jit(solution)/shard_map/ppermute | solution.py:240
  6.8 37.7 %collective-permute-start.5 = (bf16[128,768]{1,0:T(8,128)(2,1)S(1)}, bf16[128,768]{1,0:T(8,128)(2,1)S(1)}, u32[]{:S(2)}, u32[]{:S(2)}) collective-permute-start(bf16[128,768]{1,0:T(8,128)(2,1)S(1)} %pick.1), channel_id=1, source_target_pairs={{0,6},{2,4},{4,2},{6,0},{1,7},{3,5},{5,3},{7,1},{8,14},{10,12},{12... | collective-permute-start | bytes 589832 | tf_op jit(solution)/shard_map/ppermute | solution.py:240
  9.5 49.7 %collective-permute-start.11 = (bf16[96,1536]{1,0:T(8,128)(2,1)S(1)}, bf16[96,1536]{1,0:T(8,128)(2,1)S(1)}, u32[]{:S(2)}, u32[]{:S(2)}) collective-permute-start(bf16[96,1536]{1,0:T(8,128)(2,1)S(1)} %get-tuple-element.18), channel_id=1, source_target_pairs={{0,6},{2,4},{4,2},{6,0},{1,7},{3,5},{5,3},{7,1},{8,14},{10,12},{12... | collective-permute-start | bytes 884744 | tf_op jit(solution)/shard_map/ppermute | solution.py:240
  10.1 49.1 %collective-permute-start.9 = (bf16[96,1536]{1,0:T(8,128)(2,1)S(1)}, bf16[96,1536]{1,0:T(8,128)(2,1)S(1)}, u32[]{:S(2)}, u32[]{:S(2)}) collective-permute-start(bf16[96,1536]{1,0:T(8,128)(2,1)S(1)} %get-tuple-element.19), channel_id=1, source_target_pairs={{0,2},{2,0},{4,6},{6,4},{1,3},{3,1},{5,7},{7,5},{8,10},{10,8},{12,... | collective-permute-start | bytes 884744 | tf_op jit(solution)/shard_map/ppermute | solution.py:240
  13.8 48.2 %copy-start = (bf16[1,512,768]{2,1,0:T(8,128)(2,1)S(1)}, bf16[1,512,768]{2,1,0:T(8,128)(2,1)}, u32[]{:S(2)}) copy-start(bf16[1,512,768]{2,1,0:T(8,128)(2,1)} %param.9) | copy-start | bytes 2359300
  39.2 28.0 %collective-permute-start.6 = (bf16[128,768]{1,0:T(8,128)(2,1)S(1)}, bf16[128,768]{1,0:T(8,128)(2,1)S(1)}, u32[]{:S(2)}, u32[]{:S(2)}) collective-permute-start(bf16[128,768]{1,0:T(8,128)(2,1)S(1)} %get-tuple-element.23), channel_id=1, source_target_pairs={{0,2},{2,0},{4,6},{6,4},{1,3},{3,1},{5,7},{7,5},{8,10},{10,8},{12,... | collective-permute-start | bytes 589832 | tf_op jit(solution)/shard_map/ppermute | solution.py:240
  44.4 22.9 %collective-permute-start.7 = (bf16[128,768]{1,0:T(8,128)(2,1)S(1)}, bf16[128,768]{1,0:T(8,128)(2,1)S(1)}, u32[]{:S(2)}, u32[]{:S(2)}) collective-permute-start(bf16[128,768]{1,0:T(8,128)(2,1)S(1)} %get-tuple-element.25), channel_id=1, source_target_pairs={{0,4},{2,6},{4,0},{6,2},{1,5},{3,7},{5,1},{7,3},{8,12},{10,14},{12... | collective-permute-start | bytes 589832 | tf_op jit(solution)/shard_map/ppermute | solution.py:240
  44.4 27.4 %collective-permute-start.8 = (bf16[128,768]{1,0:T(8,128)(2,1)S(1)}, bf16[128,768]{1,0:T(8,128)(2,1)S(1)}, u32[]{:S(2)}, u32[]{:S(2)}) collective-permute-start(bf16[128,768]{1,0:T(8,128)(2,1)S(1)} %get-tuple-element.22), channel_id=1, source_target_pairs={{0,6},{2,4},{4,2},{6,0},{1,7},{3,5},{5,3},{7,1},{8,14},{10,12},{12... | collective-permute-start | bytes 589832 | tf_op jit(solution)/shard_map/ppermute | solution.py:240
  59.2 15.0 %collective-permute-start = (bf16[128,768]{1,0:T(8,128)(2,1)S(1)}, bf16[128,768]{1,0:T(8,128)(2,1)S(1)}, u32[]{:S(2)}, u32[]{:S(2)}) collective-permute-start(bf16[128,768]{1,0:T(8,128)(2,1)S(1)} %get-tuple-element.30), channel_id=1, source_target_pairs={{0,2},{2,0},{4,6},{6,4},{1,3},{3,1},{5,7},{7,5},{8,10},{10,8},{12,... | collective-permute-start | bytes 589832 | tf_op jit(solution)/shard_map/ppermute | solution.py:240
  59.2 31.1 %collective-permute-start.1 = (bf16[128,768]{1,0:T(8,128)(2,1)S(1)}, bf16[128,768]{1,0:T(8,128)(2,1)S(1)}, u32[]{:S(2)}, u32[]{:S(2)}) collective-permute-start(bf16[128,768]{1,0:T(8,128)(2,1)S(1)} %get-tuple-element.32), channel_id=1, source_target_pairs={{0,4},{2,6},{4,0},{6,2},{1,5},{3,7},{5,1},{7,3},{8,12},{10,14},{12... | collective-permute-start | bytes 589832 | tf_op jit(solution)/shard_map/ppermute | solution.py:240
  67.2 39.5 %collective-permute-start.12 = (bf16[96,1536]{1,0:T(8,128)(2,1)S(1)}, bf16[96,1536]{1,0:T(8,128)(2,1)S(1)}, u32[]{:S(2)}, u32[]{:S(2)}) collective-permute-start(bf16[96,1536]{1,0:T(8,128)(2,1)S(1)} %get-tuple-element.14), channel_id=1, source_target_pairs={{2,0},{0,2},{6,4},{4,6},{3,1},{1,3},{7,5},{5,7},{10,8},{8,10},{14,... | collective-permute-start | bytes 884744 | tf_op jit(solution)/shard_map/ppermute | solution.py:248
  67.3 39.4 %collective-permute-start.13 = (bf16[96,1536]{1,0:T(8,128)(2,1)S(1)}, bf16[96,1536]{1,0:T(8,128)(2,1)S(1)}, u32[]{:S(2)}, u32[]{:S(2)}) collective-permute-start(bf16[96,1536]{1,0:T(8,128)(2,1)S(1)} %get-tuple-element.15), channel_id=1, source_target_pairs={{4,0},{6,2},{0,4},{2,6},{5,1},{7,3},{1,5},{3,7},{12,8},{14,10},{8,... | collective-permute-start | bytes 884744 | tf_op jit(solution)/shard_map/ppermute | solution.py:248
  71.9 31.6 %collective-permute-start.2 = (bf16[128,768]{1,0:T(8,128)(2,1)S(1)}, bf16[128,768]{1,0:T(8,128)(2,1)S(1)}, u32[]{:S(2)}, u32[]{:S(2)}) collective-permute-start(bf16[128,768]{1,0:T(8,128)(2,1)S(1)} %get-tuple-element.29), channel_id=1, source_target_pairs={{0,6},{2,4},{4,2},{6,0},{1,7},{3,5},{5,3},{7,1},{8,14},{10,12},{12... | collective-permute-start | bytes 589832 | tf_op jit(solution)/shard_map/ppermute | solution.py:240
  74.2 32.5 %collective-permute-start.14 = (bf16[96,768]{1,0:T(8,128)(2,1)S(1)}, bf16[96,768]{1,0:T(8,128)(2,1)S(1)}, u32[]{:S(2)}, u32[]{:S(2)}) collective-permute-start(bf16[96,768]{1,0:T(8,128)(2,1)S(1)} %get-tuple-element.16), channel_id=1, source_target_pairs={{6,0},{4,2},{2,4},{0,6},{7,1},{5,3},{3,5},{1,7},{14,8},{12,10},{10... | collective-permute-start | bytes 442376 | tf_op jit(solution)/shard_map/ppermute | solution.py:248
  90.2 18.2 %collective-permute-start.15 = (bf16[96,768]{1,0:T(8,128)(2,1)S(1)}, bf16[96,768]{1,0:T(8,128)(2,1)S(1)}, u32[]{:S(2)}, u32[]{:S(2)}) collective-permute-start(bf16[96,768]{1,0:T(8,128)(2,1)S(1)} %get-tuple-element.17), channel_id=1, source_target_pairs={{6,0},{4,2},{2,4},{0,6},{7,1},{5,3},{3,5},{1,7},{14,8},{12,10},{10... | collective-permute-start | bytes 442376 | tf_op jit(solution)/shard_map/ppermute | solution.py:248

commit v4 on v2

--- a/solution.py
+++ b/solution.py
@@ -199,12 +199,13 @@
 
 
 def send_order(count):
-    near, far = [1], list(range(count - 1, 1, -1))
-    first = [(name, step) for step in far[:1] for name in ("query", "text")]
-    first += [(name, step) for step in near for name in ("query", "text", "key", "value")]
-    later = [(name, step) for name in ("query", "text") for step in far[1:]]
-    later += [(name, step) for name in ("key", "value") for step in far]
-    return first + later
+    steps = range(count - 1, 0, -1)
+    return [
+        (name, step)
+        for names in (("query", "text"), ("key", "value"))
+        for step in steps
+        for name in names
+    ]
 
 
 def solution(mesh):

time: 112 us -> 112 us (level)
  no operation moved by 1% of the time
where the time goes in v4:
time: 112 us
  waiting for transfers between devices  64.7 us (58%)
  starting transfers between devices  30.9 us (28%)
  Pallas kernels  11.8 us (11%)
  local copies, waits for them, and re-layouts  3.81 us (3%)
    ppermute x12, waiting for transfers between devices, per_device(): lax.ppermute(columns(name, step) if at else held, 'head', [(index, target...  64.7 us
    ppermute x12, starting transfers between devices, per_device(): lax.ppermute(columns(name, step) if at else held, 'head', [(index, target...  26.5 us
    pallas_call x3, Pallas kernels, vmem_call(): pl.pallas_call(kernel, out_shape=out_shape, in_specs=[spec] * len(operand...  9.25 us
    ppermute x3, starting transfers between devices, per_device(): lax.ppermute(grad_pieces[step], 'head', [(target(index, step), index) for...  4.44 us
    dynamic_slice x4, local copies, waits for them, and re-layouts, columns(): return lax.dynamic_slice(arrays[name], (0, at), (rows, width))  2.96 us
  transfers between devices with their start and end apart: 15, of which 4 were waited for; matrix products, arithmetic and copies ran while one was open for 2% of the time, Pallas kernels for 10%

profile of v4, /device:TPU:0, one launch (start us, length us, event | category | flops | bytes accessed | tf_op | source)
XLA Modules:
  0.0 112.0 jit_solution(7606477412567402744)
XLA Ops:
  0.6 0.0 copy-start.1
  0.6 0.0 copy-start.2
  0.7 1.1 pick.1
  1.8 0.1 copy-done.1
  1.9 0.7 constant_dynamic-slice_fusion
  2.6 3.1 %collective-permute-start.3 = (bf16[128,768]{1,0:T(8,128)(2,1)}, bf16[128,768]{1,0:T(8,128)(2,1)S(1)}, u32[]{:S(2)}, u32[]{:S(2)}) collective-permute-start(bf16[128,768]{1,0:T(8,128)(2,1)} %get-tuple-element.25), channel_id=1, source_target_pairs={{0,2},{2,0},{4,6},{6,4},{1,3},{3,1},{5,7},{7,5},{8,10},{10,8},{12,... | collective-permute-start | bytes 589832 | tf_op jit(solution)/shard_map/ppermute | solution.py:237
  5.6 2.6 %collective-permute-start.4 = (bf16[128,768]{1,0:T(8,128)(2,1)S(1)}, bf16[128,768]{1,0:T(8,128)(2,1)S(1)}, u32[]{:S(2)}, u32[]{:S(2)}) collective-permute-start(bf16[128,768]{1,0:T(8,128)(2,1)S(1)} %get-tuple-element.24), channel_id=1, source_target_pairs={{0,4},{2,6},{4,0},{6,2},{1,5},{3,7},{5,1},{7,3},{8,12},{10,14},{12... | collective-permute-start | bytes 589832 | tf_op jit(solution)/shard_map/ppermute | solution.py:237
  8.2 0.0 collective-permute-start.5
  8.2 0.0 copy-done.2
  8.2 0.9 dynamic-slice_bitcast_fusion
  9.1 1.9 %collective-permute-start.10 = (bf16[96,1536]{1,0:T(8,128)(2,1)}, bf16[96,1536]{1,0:T(8,128)(2,1)S(1)}, u32[]{:S(2)}, u32[]{:S(2)}) collective-permute-start(bf16[96,1536]{1,0:T(8,128)(2,1)} %get-tuple-element.19), channel_id=1, source_target_pairs={{0,4},{2,6},{4,0},{6,2},{1,5},{3,7},{5,1},{7,3},{8,12},{10,14},{12... | collective-permute-start | bytes 884744 | tf_op jit(solution)/shard_map/ppermute | solution.py:237
  11.0 1.9 %collective-permute-start.11 = (bf16[96,1536]{1,0:T(8,128)(2,1)}, bf16[96,1536]{1,0:T(8,128)(2,1)S(1)}, u32[]{:S(2)}, u32[]{:S(2)}) collective-permute-start(bf16[96,1536]{1,0:T(8,128)(2,1)} %get-tuple-element.16), channel_id=1, source_target_pairs={{0,6},{2,4},{4,2},{6,0},{1,7},{3,5},{5,3},{7,1},{8,14},{10,12},{12... | collective-permute-start | bytes 884744 | tf_op jit(solution)/shard_map/ppermute | solution.py:237
  12.9 1.4 %collective-permute-done.3.refs_1_ = bf16[128,768]{1,0:T(8,128)(2,1)S(1)} collective-permute-done((bf16[128,768]{1,0:T(8,128)(2,1)}, bf16[128,768]{1,0:T(8,128)(2,1)S(1)}, u32[]{:S(2)}, u32[]{:S(2)}) %collective-permute-start.3) | collective-permute-done | bytes 196640 | tf_op jit(solution)/shard_map/ppermute | solution.py:237
  14.3 0.0 collective-permute-start.9
  14.3 1.3 %dynamic-slice_bitcast_fusion.4 = (bf16[128,768]{1,0:T(8,128)(2,1)S(1)}, bf16[128,768]{1,0:T(8,128)(2,1)S(1)}, bf16[128,768]{1,0:T(8,128)(2,1)S(1)}, bf16[128,768]{1,0:T(8,128)(2,1)S(1)}) fusion(bf16[1,128,3072]{2,1,0:T(8,128)(2,1)} %param.6, s32[]{:T(128)S(6)} %select_n.35, s32[]{:T(128)S(6)} %select_n.33, s32[]{:T(128)S(6)} %select_n.32, s32[]{:T(128)S(6)} %select_n.34), kind=kLoop, calls=%fused_computation.5 | loop fusion | bytes 1572880 | tf_op jit(solution)/shard_map/dynamic_slice | solution.py:230
  15.6 0.0 copy-start
  15.6 19.9 %collective-permute-done.4.refs_2_ = bf16[128,768]{1,0:T(8,128)(2,1)S(1)} collective-permute-done((bf16[128,768]{1,0:T(8,128)(2,1)S(1)}, bf16[128,768]{1,0:T(8,128)(2,1)S(1)}, u32[]{:S(2)}, u32[]{:S(2)}) %collective-permute-start.4) | collective-permute-done | bytes 196640 | tf_op jit(solution)/shard_map/ppermute | solution.py:237
  35.5 0.0 collective-permute-start.6
  35.5 0.0 collective-permute-done.5.refs_3_
  35.5 5.8 %collective-permute-start.7 = (bf16[128,768]{1,0:T(8,128)(2,1)S(1)}, bf16[128,768]{1,0:T(8,128)(2,1)S(1)}, u32[]{:S(2)}, u32[]{:S(2)}) collective-permute-start(bf16[128,768]{1,0:T(8,128)(2,1)S(1)} %get-tuple-element.23), channel_id=1, source_target_pairs={{0,4},{2,6},{4,0},{6,2},{1,5},{3,7},{5,1},{7,3},{8,12},{10,14},{12... | collective-permute-start | bytes 589832 | tf_op jit(solution)/shard_map/ppermute | solution.py:237
  41.2 0.0 copy-done.3
  41.2 0.1 dynamic-slice_bitcast_fusion.8
  41.3 11.0 %collective-permute-done.10.refs_6_ = bf16[96,1536]{1,0:T(8,128)(2,1)S(1)} collective-permute-done((bf16[96,1536]{1,0:T(8,128)(2,1)}, bf16[96,1536]{1,0:T(8,128)(2,1)S(1)}, u32[]{:S(2)}, u32[]{:S(2)}) %collective-permute-start.10) | collective-permute-done | bytes 294944 | tf_op jit(solution)/shard_map/ppermute | solution.py:237
  52.4 2.5 %collective-permute-start.8 = (bf16[128,768]{1,0:T(8,128)(2,1)S(1)}, bf16[128,768]{1,0:T(8,128)(2,1)S(1)}, u32[]{:S(2)}, u32[]{:S(2)}) collective-permute-start(bf16[128,768]{1,0:T(8,128)(2,1)S(1)} %get-tuple-element.20), channel_id=1, source_target_pairs={{0,6},{2,4},{4,2},{6,0},{1,7},{3,5},{5,3},{7,1},{8,14},{10,12},{12... | collective-permute-start | bytes 589832 | tf_op jit(solution)/shard_map/ppermute | solution.py:237
  54.8 0.0 collective-permute-done.11.refs_7_
  54.8 6.5 %collective-permute-start = (bf16[128,768]{1,0:T(8,128)(2,1)S(1)}, bf16[128,768]{1,0:T(8,128)(2,1)S(1)}, u32[]{:S(2)}, u32[]{:S(2)}) collective-permute-start(bf16[128,768]{1,0:T(8,128)(2,1)S(1)} %get-tuple-element.28), channel_id=1, source_target_pairs={{0,2},{2,0},{4,6},{6,4},{1,3},{3,1},{5,7},{7,5},{8,10},{10,8},{12,... | collective-permute-start | bytes 589832 | tf_op jit(solution)/shard_map/ppermute | solution.py:237
  61.3 0.0 collective-permute-done.9.refs_5_
  61.4 0.0 copy-done
  61.4 5.2 %shard_map.69 = (f32[512,768]{1,0:T(8,128)S(1)}, bf16[96,1536]{1,0:T(8,128)(2,1)S(1)}, bf16[96,1536]{1,0:T(8,128)(2,1)S(1)}, bf16[96,1536]{1,0:T(8,128)(2,1)S(1)}, bf16[96,1536]{1,0:T(8,128)(2,1)S(1)}) custom-call(bf16[128,768]{1,0:T(8,128)(2,1)S(1)} %get-tuple-element.26.refs_0_, bf16[128,768]{1,0:T(8,128)(2,1)S(1)} %collective-permute-done.3.refs_1_, ...), custom_call_target="tpu_custom_call" | custom-call | tf_op jit(solution)/shard_map/pallas_call | solution.py:103
  66.5 0.1 collective-permute-start.12
  66.6 0.0 collective-permute-done.6.refs_5_
  66.6 2.7 %collective-permute-start.13 = (bf16[96,1536]{1,0:T(8,128)(2,1)S(1)}, bf16[96,1536]{1,0:T(8,128)(2,1)S(1)}, u32[]{:S(2)}, u32[]{:S(2)}) collective-permute-start(bf16[96,1536]{1,0:T(8,128)(2,1)S(1)} %get-tuple-element.14), channel_id=1, source_target_pairs={{4,0},{6,2},{0,4},{2,6},{5,1},{7,3},{1,5},{3,7},{12,8},{14,10},{8,... | collective-permute-start | bytes 884744 | tf_op jit(solution)/shard_map/ppermute | solution.py:246
  69.3 0.0 collective-permute-done.7.refs_6_
  69.3 1.7 %collective-permute-start.14 = (bf16[96,1536]{1,0:T(8,128)(2,1)S(1)}, bf16[96,1536]{1,0:T(8,128)(2,1)S(1)}, u32[]{:S(2)}, u32[]{:S(2)}) collective-permute-start(bf16[96,1536]{1,0:T(8,128)(2,1)S(1)} %get-tuple-element.15), channel_id=1, source_target_pairs={{6,0},{4,2},{2,4},{0,6},{7,1},{5,3},{3,5},{1,7},{14,8},{12,10},{10... | collective-permute-start | bytes 884744 | tf_op jit(solution)/shard_map/ppermute | solution.py:246
  71.0 0.0 collective-permute-done.8.refs_7_
  71.0 0.4 collective-permute-start.1
  71.4 0.0 collective-permute-done.refs_1_
  71.4 1.9 %collective-permute-start.2 = (bf16[128,768]{1,0:T(8,128)(2,1)S(1)}, bf16[128,768]{1,0:T(8,128)(2,1)S(1)}, u32[]{:S(2)}, u32[]{:S(2)}) collective-permute-start(bf16[128,768]{1,0:T(8,128)(2,1)S(1)} %get-tuple-element.27), channel_id=1, source_target_pairs={{0,6},{2,4},{4,2},{6,0},{1,7},{3,5},{5,3},{7,1},{8,14},{10,12},{12... | collective-permute-start | bytes 589832 | tf_op jit(solution)/shard_map/ppermute | solution.py:237
  73.2 0.1 pad_add_fusion.refs_0_
  73.3 2.2 %shard_map.68.refs_4_ = bf16[512,3072]{1,0:T(8,128)(2,1)S(1)} custom-call(bf16[128,768]{1,0:T(8,128)(2,1)S(1)} %get-tuple-element.26.refs_0_, bf16[128,768]{1,0:T(8,128)(2,1)S(1)} %collective-permute-done.3.refs_1_, bf16[128,768]{1,0:T(8,128)(2,1)S(1)} %collective-permute-done.4.refs_2_, bf16[128,768]{1,0:T(8,128)(2,1)S(1)} %collective-permute-done.5.refs_3_, ...), custom_call_target="tpu_custom_call" | custom-call | tf_op jit(solution)/shard_map/pallas_call | solution.py:103
  75.5 32.4 %collective-permute-done.1.refs_2_ = bf16[128,768]{1,0:T(8,128)(2,1)S(1)} collective-permute-done((bf16[128,768]{1,0:T(8,128)(2,1)S(1)}, bf16[128,768]{1,0:T(8,128)(2,1)S(1)}, u32[]{:S(2)}, u32[]{:S(2)}) %collective-permute-start.1) | collective-permute-done | bytes 196640 | tf_op jit(solution)/shard_map/ppermute | solution.py:237
  107.9 0.0 collective-permute-done.2.refs_3_
  107.9 1.9 %shard_map.70 = bf16[512,768]{1,0:T(8,128)(2,1)} custom-call(bf16[128,768]{1,0:T(8,128)(2,1)S(1)} %get-tuple-element.29.refs_0_, bf16[128,768]{1,0:T(8,128)(2,1)S(1)} %collective-permute-done.refs_1_, bf16[128,768]{1,0:T(8,128)(2,1)S(1)} %collective-permute-done.1.refs_2_, bf16[128,768]{1,0:T(8,128)(2,1)S(1)} %collective-permute-done.2.refs_3_, ...), custom_call_target="tpu_custom_call" | custom-call | tf_op jit(solution)/shard_map/pallas_call | solution.py:103
  109.8 0.0 collective-permute-done.12.refs_2_
  109.8 0.0 collective-permute-done.13.refs_3_
  109.8 1.5 %place.1 = bf16[96,6144]{1,0:T(8,128)(2,1)} custom-call(s32[4]{0:T(128)S(1)} %pad_add_fusion.refs_0_, bf16[96,1536]{1,0:T(8,128)(2,1)S(1)} %get-tuple-element.12.refs_1_, bf16[96,1536]{1,0:T(8,128)(2,1)S(1)} %collective-permute-done.12.refs_2_, bf16[96,1536]{1,0:T(8,128)(2,1)S(1)} %collective-permute-done.13.refs_3_), custom_call_target="tpu_custom_call" | custom-call | tf_op jit(solution)/shard_map/place/pallas_call | solution.py:166
  111.3 0.0 collective-permute-done.14
  111.3 0.7 bitcast_dynamic-update-slice_fusion
  (1 shorter events, 0.0 us)
Async XLA Ops:
  0.6 1.2 %copy-start.1 = (bf16[1,128,3072]{2,1,0:T(8,128)(2,1)S(1)}, bf16[1,128,3072]{2,1,0:T(8,128)(2,1)}, u32[]{:S(2)}) copy-start(bf16[1,128,3072]{2,1,0:T(8,128)(2,1)} %param.5) | copy-start | bytes 2359300
  0.6 7.6 %copy-start.2 = (bf16[1,96,6144]{2,1,0:T(8,128)(2,1)S(1)}, bf16[1,96,6144]{2,1,0:T(8,128)(2,1)}, u32[]{:S(2)}) copy-start(bf16[1,96,6144]{2,1,0:T(8,128)(2,1)} %param.8) | copy-start | bytes 3538948
  2.6 11.7 %collective-permute-start.3 = (bf16[128,768]{1,0:T(8,128)(2,1)}, bf16[128,768]{1,0:T(8,128)(2,1)S(1)}, u32[]{:S(2)}, u32[]{:S(2)}) collective-permute-start(bf16[128,768]{1,0:T(8,128)(2,1)} %get-tuple-element.25), channel_id=1, source_target_pairs={{0,2},{2,0},{4,6},{6,4},{1,3},{3,1},{5,7},{7,5},{8,10},{10,8},{12,... | collective-permute-start | bytes 589832 | tf_op jit(solution)/shard_map/ppermute | solution.py:237
  5.6 29.8 %collective-permute-start.4 = (bf16[128,768]{1,0:T(8,128)(2,1)S(1)}, bf16[128,768]{1,0:T(8,128)(2,1)S(1)}, u32[]{:S(2)}, u32[]{:S(2)}) collective-permute-start(bf16[128,768]{1,0:T(8,128)(2,1)S(1)} %get-tuple-element.24), channel_id=1, source_target_pairs={{0,4},{2,6},{4,0},{6,2},{1,5},{3,7},{5,1},{7,3},{8,12},{10,14},{12... | collective-permute-start | bytes 589832 | tf_op jit(solution)/shard_map/ppermute | solution.py:237
  8.2 27.2 %collective-permute-start.5 = (bf16[128,768]{1,0:T(8,128)(2,1)S(1)}, bf16[128,768]{1,0:T(8,128)(2,1)S(1)}, u32[]{:S(2)}, u32[]{:S(2)}) collective-permute-start(bf16[128,768]{1,0:T(8,128)(2,1)S(1)} %pick.1), channel_id=1, source_target_pairs={{0,6},{2,4},{4,2},{6,0},{1,7},{3,5},{5,3},{7,1},{8,14},{10,12},{12... | collective-permute-start | bytes 589832 | tf_op jit(solution)/shard_map/ppermute | solution.py:237
  9.1 32.1 %copy-start.3 = (bf16[1,128,3072]{2,1,0:T(8,128)(2,1)S(1)}, bf16[1,128,3072]{2,1,0:T(8,128)(2,1)}, u32[]{:S(2)}) copy-start(bf16[1,128,3072]{2,1,0:T(8,128)(2,1)} %param.7) | copy-start | bytes 2359300
  9.1 43.2 %collective-permute-start.10 = (bf16[96,1536]{1,0:T(8,128)(2,1)}, bf16[96,1536]{1,0:T(8,128)(2,1)S(1)}, u32[]{:S(2)}, u32[]{:S(2)}) collective-permute-start(bf16[96,1536]{1,0:T(8,128)(2,1)} %get-tuple-element.19), channel_id=1, source_target_pairs={{0,4},{2,6},{4,0},{6,2},{1,5},{3,7},{5,1},{7,3},{8,12},{10,14},{12... | collective-permute-start | bytes 884744 | tf_op jit(solution)/shard_map/ppermute | solution.py:237
  11.0 43.8 %collective-permute-start.11 = (bf16[96,1536]{1,0:T(8,128)(2,1)}, bf16[96,1536]{1,0:T(8,128)(2,1)S(1)}, u32[]{:S(2)}, u32[]{:S(2)}) collective-permute-start(bf16[96,1536]{1,0:T(8,128)(2,1)} %get-tuple-element.16), channel_id=1, source_target_pairs={{0,6},{2,4},{4,2},{6,0},{1,7},{3,5},{5,3},{7,1},{8,14},{10,12},{12... | collective-permute-start | bytes 884744 | tf_op jit(solution)/shard_map/ppermute | solution.py:237
  14.3 47.0 %collective-permute-start.9 = (bf16[96,1536]{1,0:T(8,128)(2,1)S(1)}, bf16[96,1536]{1,0:T(8,128)(2,1)S(1)}, u32[]{:S(2)}, u32[]{:S(2)}) collective-permute-start(bf16[96,1536]{1,0:T(8,128)(2,1)S(1)} %get-tuple-element.17), channel_id=1, source_target_pairs={{0,2},{2,0},{4,6},{6,4},{1,3},{3,1},{5,7},{7,5},{8,10},{10,8},{12,... | collective-permute-start | bytes 884744 | tf_op jit(solution)/shard_map/ppermute | solution.py:237
  15.6 45.8 %copy-start = (bf16[1,512,768]{2,1,0:T(8,128)(2,1)S(1)}, bf16[1,512,768]{2,1,0:T(8,128)(2,1)}, u32[]{:S(2)}) copy-start(bf16[1,512,768]{2,1,0:T(8,128)(2,1)} %param.9) | copy-start | bytes 2359300
  35.5 31.2 %collective-permute-start.6 = (bf16[128,768]{1,0:T(8,128)(2,1)S(1)}, bf16[128,768]{1,0:T(8,128)(2,1)S(1)}, u32[]{:S(2)}, u32[]{:S(2)}) collective-permute-start(bf16[128,768]{1,0:T(8,128)(2,1)S(1)} %get-tuple-element.21), channel_id=1, source_target_pairs={{0,2},{2,0},{4,6},{6,4},{1,3},{3,1},{5,7},{7,5},{8,10},{10,8},{12,... | collective-permute-start | bytes 589832 | tf_op jit(solution)/shard_map/ppermute | solution.py:237
  35.5 33.9 %collective-permute-start.7 = (bf16[128,768]{1,0:T(8,128)(2,1)S(1)}, bf16[128,768]{1,0:T(8,128)(2,1)S(1)}, u32[]{:S(2)}, u32[]{:S(2)}) collective-permute-start(bf16[128,768]{1,0:T(8,128)(2,1)S(1)} %get-tuple-element.23), channel_id=1, source_target_pairs={{0,4},{2,6},{4,0},{6,2},{1,5},{3,7},{5,1},{7,3},{8,12},{10,14},{12... | collective-permute-start | bytes 589832 | tf_op jit(solution)/shard_map/ppermute | solution.py:237
  52.4 18.6 %collective-permute-start.8 = (bf16[128,768]{1,0:T(8,128)(2,1)S(1)}, bf16[128,768]{1,0:T(8,128)(2,1)S(1)}, u32[]{:S(2)}, u32[]{:S(2)}) collective-permute-start(bf16[128,768]{1,0:T(8,128)(2,1)S(1)} %get-tuple-element.20), channel_id=1, source_target_pairs={{0,6},{2,4},{4,2},{6,0},{1,7},{3,5},{5,3},{7,1},{8,14},{10,12},{12... | collective-permute-start | bytes 589832 | tf_op jit(solution)/shard_map/ppermute | solution.py:237
  54.8 16.5 %collective-permute-start = (bf16[128,768]{1,0:T(8,128)(2,1)S(1)}, bf16[128,768]{1,0:T(8,128)(2,1)S(1)}, u32[]{:S(2)}, u32[]{:S(2)}) collective-permute-start(bf16[128,768]{1,0:T(8,128)(2,1)S(1)} %get-tuple-element.28), channel_id=1, source_target_pairs={{0,2},{2,0},{4,6},{6,4},{1,3},{3,1},{5,7},{7,5},{8,10},{10,8},{12,... | collective-permute-start | bytes 589832 | tf_op jit(solution)/shard_map/ppermute | solution.py:237
  66.5 43.2 %collective-permute-start.12 = (bf16[96,1536]{1,0:T(8,128)(2,1)S(1)}, bf16[96,1536]{1,0:T(8,128)(2,1)S(1)}, u32[]{:S(2)}, u32[]{:S(2)}) collective-permute-start(bf16[96,1536]{1,0:T(8,128)(2,1)S(1)} %get-tuple-element.13), channel_id=1, source_target_pairs={{2,0},{0,2},{6,4},{4,6},{3,1},{1,3},{7,5},{5,7},{10,8},{8,10},{14,... | collective-permute-start | bytes 884744 | tf_op jit(solution)/shard_map/ppermute | solution.py:246
  66.6 43.2 %collective-permute-start.13 = (bf16[96,1536]{1,0:T(8,128)(2,1)S(1)}, bf16[96,1536]{1,0:T(8,128)(2,1)S(1)}, u32[]{:S(2)}, u32[]{:S(2)}) collective-permute-start(bf16[96,1536]{1,0:T(8,128)(2,1)S(1)} %get-tuple-element.14), channel_id=1, source_target_pairs={{4,0},{6,2},{0,4},{2,6},{5,1},{7,3},{1,5},{3,7},{12,8},{14,10},{8,... | collective-permute-start | bytes 884744 | tf_op jit(solution)/shard_map/ppermute | solution.py:246
  69.3 42.0 %collective-permute-start.14 = (bf16[96,1536]{1,0:T(8,128)(2,1)S(1)}, bf16[96,1536]{1,0:T(8,128)(2,1)S(1)}, u32[]{:S(2)}, u32[]{:S(2)}) collective-permute-start(bf16[96,1536]{1,0:T(8,128)(2,1)S(1)} %get-tuple-element.15), channel_id=1, source_target_pairs={{6,0},{4,2},{2,4},{0,6},{7,1},{5,3},{3,5},{1,7},{14,8},{12,10},{10... | collective-permute-start | bytes 884744 | tf_op jit(solution)/shard_map/ppermute | solution.py:246
  71.0 36.9 %collective-permute-start.1 = (bf16[128,768]{1,0:T(8,128)(2,1)S(1)}, bf16[128,768]{1,0:T(8,128)(2,1)S(1)}, u32[]{:S(2)}, u32[]{:S(2)}) collective-permute-start(bf16[128,768]{1,0:T(8,128)(2,1)S(1)} %get-tuple-element.30), channel_id=1, source_target_pairs={{0,4},{2,6},{4,0},{6,2},{1,5},{3,7},{5,1},{7,3},{8,12},{10,14},{12... | collective-permute-start | bytes 589832 | tf_op jit(solution)/shard_map/ppermute | solution.py:237
  71.4 36.5 %collective-permute-start.2 = (bf16[128,768]{1,0:T(8,128)(2,1)S(1)}, bf16[128,768]{1,0:T(8,128)(2,1)S(1)}, u32[]{:S(2)}, u32[]{:S(2)}) collective-permute-start(bf16[128,768]{1,0:T(8,128)(2,1)S(1)} %get-tuple-element.27), channel_id=1, source_target_pairs={{0,6},{2,4},{4,2},{6,0},{1,7},{3,5},{5,3},{7,1},{8,14},{10,12},{12... | collective-permute-start | bytes 589832 | tf_op jit(solution)/shard_map/ppermute | solution.py:237
